TPU v7x, 32 devices: a whole 2x2x4 slice. The times are simulated.
32 devices in a mesh: region: 8 (over z, core), head: 4 (over y, x).
Axes of the slice: x: 2, y: 2, z: 4, core: 2. Of those that a mesh axis runs over, the one named last changes fastest.
Arguments:
- fine_tokens: float32 [18432, 512], P(('region', 'head')), may hold values from -6 to 6
- fine_shift: int32 [1], replicated, may hold values from 1 to 143
- window_counts: int32 [32], P('region'), may hold values from 36 to 144
- fine_qkv: bfloat16 [512, 1536], replicated, may hold values from -4 to 4
- fine_proj: bfloat16 [512, 512], replicated, may hold values from -0.25 to 0.25
- fine_up: bfloat16 [512, 2048], replicated, may hold values from -0.25 to 0.25
- fine_down: bfloat16 [2048, 512], replicated, may hold values from -0.125 to 0.125
- merge_weight: bfloat16 [2048, 1024], replicated, may hold values from -0.125 to 0.125
- coarse_qkv: bfloat16 [1024, 3072], P('region', 'head'), may hold values from -4 to 4
- coarse_proj: bfloat16 [1024, 1024], P('head', 'region'), may hold values from -0.1875 to 0.1875
- coarse_up: bfloat16 [1024, 4096], P('region', 'head'), may hold values from -0.1875 to 0.1875
- coarse_down: bfloat16 [4096, 1024], P('head', 'region'), may hold values from -0.09375 to 0.09375
- expand_weight: bfloat16 [1024, 2048], replicated, may hold values from -0.1875 to 0.1875
- out_weight: bfloat16 [1024, 512], replicated, may hold values from -0.1875 to 0.1875
Outputs:
- fine_result: float32 [18432, 512], P(('region', 'head'))
All inputs are finite; a program needn't handle non-finite values.
Results may differ from a plain program's by a relative error of at most 0.012.
Values may be sent and summed in bfloat16 or wider, within the bound.
A program may use at most 128 MiB of HBM per device.

v0:
```python
import functools

import jax
import jax.numpy as jnp
from jax import lax
from jax.experimental import pallas as pl
from jax.experimental.pallas import tpu as pltpu
from jax.sharding import PartitionSpec as P

C = 512
HD = 64
HF = 8
WIN = 144
HEADS = HF
MESH = pl.DeviceIdType.MESH
F32 = jnp.float32
BF16 = jnp.bfloat16


def norm(values):
    average = jnp.mean(values, axis=-1, keepdims=True)
    centred = values - average
    spread = jnp.mean(centred * centred, axis=-1, keepdims=True)
    return centred * lax.rsqrt(spread + 1e-05)


def gelu(values):
    return 0.5 * values * (1.0 + lax.erf(values * (0.5**0.5)))


def dot(left, right):
    return jnp.dot(left, right, preferred_element_type=F32)


def flip(index, mask):
    result = index
    bit = 1
    while bit <= mask:
        if mask & bit:
            result = result + (1 - 2 * ((index // bit) % 2)) * bit
        bit *= 2
    return result


def attend(packed, head_count, count):
    blended = []
    for head in range(head_count):
        base = head * 3 * HD
        query = packed[:, base : base + HD]
        key = packed[:, base + HD : base + 2 * HD]
        value = packed[:, base + 2 * HD : base + 3 * HD]
        scores = lax.dot_general(
            query, key, (((1,), (1,)), ((), ())), preferred_element_type=F32
        ) * (HD**-0.5)
        if count is not None:
            place = lax.broadcasted_iota(jnp.int32, scores.shape, 1)
            scores = jnp.where(place < count, scores, -1e30)
        raised = jnp.exp(scores - jnp.max(scores, axis=-1, keepdims=True))
        weights = (raised / jnp.sum(raised, axis=-1, keepdims=True)).astype(BF16)
        blended.append(dot(weights, value).astype(BF16))
    return blended


def kernel(
    region_count, head_count,
    shift, counts, tokens, w_qkv, w_proj, w_up, w_down, w_merge,
    c_qkv, c_proj, c_up, c_down, w_expand, w_out,
    out,
    v_qkv, v_proj, v_up, v_down, v_merge, v_expand, v_out,
    g_qkv, g_proj, g_up, g_down,
    extended, rolled, packed, blended, fine, fine_bf, hidden, grouped,
    coarse, shared, c_packed, c_blended, sent_blend, got_blend, mid, c_hidden, parts, got_parts, spread, lanes,
    local_sem, halo_send, halo_recv, own_sem, z_send, w_recv, p_send, q_send, q_recv, x_send, x_recv,
    a_send, a_recv, b_send, b_recv, m_send, m_recv, r_send, r_recv,
):
    region, head = lax.axis_index("region"), lax.axis_index("head")
    chips = region_count // 2
    chip, core = region // 2, region % 2
    rows = tokens.shape[0]
    blocks = rows // WIN
    flat = region * head_count + head
    total = region_count * head_count
    before, after = (flat + total - 1) % total, (flat + 1) % total
    before = (before // head_count, before % head_count)
    after = (after // head_count, after % head_count)
    partner = (chip * 2 + 1 - core, head)
    column = [(((chip + s) % chips) * 2 + core, head) for s in range(chips)]
    plane = [(region, flip(head, k)) for k in range(head_count)]

    barrier = pltpu.get_barrier_semaphore()
    greeted = [before, after, partner] + column[1:] + plane[1:]
    for device in greeted:
        pl.semaphore_signal(barrier, inc=1, device_id=device, device_id_type=MESH)

    own = []
    for at, (source, target) in enumerate(
        [(w_qkv, v_qkv), (w_proj, v_proj), (w_up, v_up), (w_down, v_down), (w_merge, v_merge),
         (w_expand, v_expand), (w_out, v_out)]
    ):
        copy = pltpu.make_async_copy(source, target, local_sem.at[at])
        copy.start()
        own.append(copy)

    shards = [c_proj, c_qkv, c_up, c_down]

    def slot(which, owner):
        if which == 0:
            return g_proj.at[head, owner]
        if which == 1:
            return g_qkv.at[pl.ds(owner * c_qkv.shape[0], c_qkv.shape[0])]
        if which == 2:
            return g_up.at[pl.ds(owner * c_up.shape[0], c_up.shape[0])]
        return g_down.at[owner]

    own_shards = []
    for which in range(4):
        copy = pltpu.make_async_copy(shards[which], slot(which, region), own_sem.at[which])
        copy.start()
        own_shards.append(copy)

    def remote(source, target, send, recv, device):
        return pltpu.make_async_remote_copy(
            src_ref=source, dst_ref=target, send_sem=send, recv_sem=recv,
            device_id=device, device_id_type=MESH,
        )

    extended[WIN : WIN + rows, :] = norm(tokens[...]).astype(BF16)
    pl.semaphore_wait(barrier, len(greeted))

    halo_left = remote(extended.at[pl.ds(WIN, WIN)], extended.at[pl.ds(WIN + rows, WIN)],
                       halo_send.at[0], halo_recv.at[0], before)
    halo_right = remote(extended.at[pl.ds(rows, WIN)], extended.at[pl.ds(0, WIN)],
                        halo_send.at[1], halo_recv.at[1], after)
    halo_left.start()
    halo_right.start()

    column_sends = []
    for which in range(4):
        for s in range(1, chips):
            copy = remote(shards[which], slot(which, region), z_send.at[which, s],
                          w_recv.at[which, region], column[s])
            copy.start()
            column_sends.append(copy)

    partner_sends = []

    def pass_on(which):
        for s in range(chips):
            owner = ((chip + s) % chips) * 2 + core
            if s == 0:
                own_shards[which].wait()
            else:
                remote(shards[which], slot(which, owner), z_send.at[which, s],
                       w_recv.at[which, owner], column[s]).wait_recv()
            copy = remote(slot(which, owner), slot(which, owner), p_send.at[which, s],
                          w_recv.at[which, owner], partner)
            copy.start()
            partner_sends.append(copy)

    def take_over(which):
        for s in range(chips):
            owner = ((chip + s) % chips) * 2 + 1 - core
            remote(slot(which, owner), slot(which, owner), p_send.at[which, s],
                   w_recv.at[which, owner], partner).wait_recv()

    relay = head_count == 4

    def gather(buffer, send, recv):
        copies = []
        for k in range(1, 3 if relay else head_count):
            piece = buffer.at[head]
            copy = remote(piece, piece, send.at[k], recv.at[k], plane[k])
            copy.start()
            copies.append(copy)
        return copies

    def far_half(buffer, mask, i, send, recv, device):
        half = buffer.shape[2] // 2
        piece = buffer.at[flip(head, mask), :, pl.ds(i * half, half)]
        return remote(piece, piece, send.at[3 * i], recv.at[3 * i], device)

    def hand_on(buffer, send, recv, copies):
        if not relay:
            return
        for i, (came, goes) in enumerate(((1, 2), (2, 1))):
            copies[came - 1].wait_recv()
            copy = far_half(buffer, came, i, send, recv, plane[goes])
            copy.start()
            copies.append(copy)

    def arrived(buffer, k, send, recv, copies):
        if not relay:
            copies[k - 1].wait_recv()
        elif k == 3:
            for i, came in enumerate((2, 1)):
                far_half(buffer, 3, i, send, recv, plane[came]).wait_recv()

    offset = shift[0]
    at_row = lax.broadcasted_iota(jnp.int32, (WIN, 2 * WIN), 0)
    at_column = lax.broadcasted_iota(jnp.int32, (WIN, 2 * WIN), 1)
    forth = (at_column == at_row + offset).astype(F32).astype(BF16)
    back = (at_column == at_row + (WIN - offset)).astype(F32).astype(BF16)
    halo_left.wait()
    halo_right.wait()
    for j in range(blocks + 1):
        rolled[j * WIN : (j + 1) * WIN, :] = dot(
            forth, extended[j * WIN : (j + 2) * WIN, :]
        ).astype(BF16)
    own[0].wait()

    def project(i, carry):
        at = pl.ds(pl.multiple_of(i * 256, 256), 256)
        packed[:, at] = dot(rolled[...], v_qkv[:, at]).astype(BF16)
        return carry

    lax.fori_loop(0, packed.shape[1] // 256, project, 0)
    pass_on(0)
    quarter = []
    for s in range(chips):
        owner = ((chip + s) % chips) * 2 + core
        for k in range(1, head_count):
            piece = g_proj.at[head, owner]
            copy = remote(piece, piece, q_send.at[k, s], q_recv.at[k, s], plane[k])
            copy.start()
            quarter.append(copy)

    def window(j, carry):
        at = pl.ds(pl.multiple_of(j * WIN, WIN), WIN)
        for half in range(2):
            width = packed.shape[1] // 2
            parts_of = attend(packed[at, half * width : (half + 1) * width], HEADS // 2, None)
            blended[at, half * (C // 2) : (half + 1) * (C // 2)] = jnp.concatenate(parts_of, axis=1)
        return carry

    lax.fori_loop(0, blocks + 1, window, 0)
    own[1].wait()
    for j in range(blocks):
        at = slice(j * WIN, (j + 1) * WIN)
        rolled[at, :] = dot(back, blended[j * WIN : (j + 2) * WIN, :]).astype(BF16)
    fine[...] = tokens[...] + dot(rolled[:rows, :], v_proj[...])
    rolled[:rows, :] = norm(fine[...]).astype(BF16)

    for s in range(chips):
        owner = ((chip + s) % chips) * 2 + core
        for k in range(1, head_count):
            piece = g_proj.at[plane[k][1], owner]
            remote(piece, piece, q_send.at[k, s], q_recv.at[k, s], plane[k]).wait_recv()
            copy = remote(piece, piece, x_send.at[k, s], x_recv.at[k, s], partner)
            copy.start()
            partner_sends.append(copy)
    own[2].wait()

    def fine_hidden(i, carry):
        at = pl.ds(pl.multiple_of(i * 256, 256), 256)
        hidden[:, at] = gelu(dot(rolled[:rows, :], v_up[:, at])).astype(BF16)
        return carry

    chunks = hidden.shape[1] // 256
    lax.fori_loop(0, chunks, fine_hidden, 0)
    own[3].wait()

    def fine_sum(i, carry):
        at = pl.ds(pl.multiple_of(i * 256, 256), 256)
        fine[:, at] += dot(hidden[...], v_down[:, at])
        return carry

    lax.fori_loop(0, C // 256, fine_sum, 0)
    pass_on(1)

    group = w_merge.shape[0] // C
    cells = rows // group
    own[4].wait()
    members = []
    for c in range(C // 128):
        lanes[c] = fine[:, c * 128 : (c + 1) * 128]
    for k in range(group):
        pieces = [lanes[c, pl.ds(k, cells, stride=group), :] for c in range(C // 128)]
        member = jnp.concatenate(pieces, axis=1)
        fine_bf[k * cells : (k + 1) * cells, :] = member.astype(BF16)
        members.append(member)
    merged = jnp.concatenate(members, axis=1)
    grouped[...] = norm(merged).astype(BF16)
    width = coarse.shape[1]

    def merge(i, carry):
        at = pl.ds(pl.multiple_of(i * 256, 256), 256)
        coarse[:, at] = dot(grouped[...], v_merge[:, at])
        return carry

    lax.fori_loop(0, width // 256, merge, 0)
    shared[head] = norm(coarse[...]).astype(BF16)
    gathers = gather(shared, a_send, a_recv)
    take_over(1)

    blends = []
    heads_here = g_qkv.shape[1] // (3 * HD)
    for k in range(head_count):
        target = plane[k][1]
        if k > 0:
            arrived(shared, k, a_send, a_recv, gathers)
        c_packed[...] = dot(shared[target], g_qkv[...]).astype(BF16)
        parts_of = attend(c_packed[...], heads_here, counts[target])
        if k == 0:
            got_blend[head] = jnp.concatenate(parts_of, axis=1)
            hand_on(shared, a_send, a_recv, gathers)
        else:
            sent_blend[k] = jnp.concatenate(parts_of, axis=1)
            copy = remote(sent_blend.at[k], got_blend.at[head], b_send.at[k], b_recv.at[k], plane[k])
            copy.start()
            blends.append(copy)
    pass_on(2)
    take_over(0)
    for s in range(chips):
        owner = ((chip + s) % chips) * 2 + 1 - core
        for k in range(1, head_count):
            piece = g_proj.at[plane[k][1], owner]
            remote(piece, piece, x_send.at[k, s], x_recv.at[k, s], partner).wait_recv()
    for copy in blends:
        copy.wait_recv()
    for r in range(region_count):
        w = g_proj.shape[3]
        total_of = dot(got_blend[0], g_proj[0, r])
        for h in range(1, head_count):
            total_of += dot(got_blend[h], g_proj[h, r])
        mid[:, r * w : (r + 1) * w] = coarse[:, r * w : (r + 1) * w] + total_of

    c_blended[head] = norm(mid[...]).astype(BF16)
    seconds = gather(c_blended, m_send, m_recv)
    take_over(2)
    pass_on(3)

    returns = []
    for k in range(head_count):
        target = plane[k][1]
        if k > 0:
            arrived(c_blended, k, m_send, m_recv, seconds)

        def coarse_hidden(i, carry):
            at = pl.ds(pl.multiple_of(i * 256, 256), 256)
            c_hidden[:, at] = gelu(dot(c_blended[target], g_up[:, at])).astype(BF16)
            return carry

        lax.fori_loop(0, c_hidden.shape[1] // 256, coarse_hidden, 0)
        if k == 0:
            hand_on(c_blended, m_send, m_recv, seconds)
            take_over(3)
        w = g_down.shape[2]
        for r in range(0, region_count, 2):
            pair = jnp.concatenate([g_down[r], g_down[r + 1]], axis=1)
            term = dot(c_hidden[...], pair)
            if k == 0:
                mid[:, r * w : (r + 2) * w] += term
            else:
                parts[k, :, r * w : (r + 2) * w] = term.astype(BF16)
        if k > 0:
            copy = remote(parts.at[k], got_parts.at[k], r_send.at[k], r_recv.at[k], plane[k])
            copy.start()
            returns.append(copy)
    own[5].wait()
    own[6].wait()
    for copy in returns:
        copy.wait_recv()
    result = mid[...]
    for k in range(1, head_count):
        result += got_parts[k].astype(F32)
    grouped[:, :width] = result.astype(BF16)
    for k in range(group):
        spread[k * cells : (k + 1) * cells, :] = dot(
            grouped[:, :width], v_expand[:, k * C : (k + 1) * C]
        ).astype(BF16)
    for c in range(C // 128):
        at = slice(c * 128, (c + 1) * 128)
        value = dot(fine_bf[...], v_out[:C, at]) + dot(spread[...], v_out[C:, at])
        for k in range(group):
            lanes[c, pl.ds(k, cells, stride=group), :] = value[k * cells : (k + 1) * cells, :]
        out[:, at] = lanes[c]

    for copy in column_sends + partner_sends + quarter + gathers + blends + seconds + returns:
        copy.wait_send()


def body(region_count, head_count, tokens, shift, counts, *weights):
    rows = tokens.shape[0]
    w_qkv, w_proj, w_up, w_down, w_merge, c_qkv, c_proj, c_up, c_down, w_expand, w_out = weights
    width = w_merge.shape[1]
    group = w_merge.shape[0] // C
    cells = rows // group
    vmem = pltpu.VMEM
    any_spec = pl.BlockSpec(memory_space=pl.ANY)
    dma = pltpu.SemaphoreType.DMA
    chips = region_count // 2
    mine = c_proj.shape[0]
    scratch = [vmem(w.shape, BF16) for w in (w_qkv, w_proj, w_up, w_down, w_merge, w_expand, w_out)]
    scratch += [
        vmem((width, c_qkv.shape[1]), BF16),
        vmem((head_count, region_count) + c_proj.shape, BF16),
        vmem((width, c_up.shape[1]), BF16),
        vmem((region_count,) + c_down.shape, BF16),
        vmem((rows + 2 * WIN, C), BF16),
        vmem((rows + WIN, C), BF16),
        vmem((rows + WIN, w_qkv.shape[1]), BF16),
        vmem((rows + WIN, C), BF16),
        vmem((rows, C), F32),
        vmem((rows, C), BF16),
        vmem((rows, w_up.shape[1]), BF16),
        vmem((cells, group * C), BF16),
        vmem((cells, width), F32),
        vmem((head_count, cells, width), BF16),
        vmem((cells, c_qkv.shape[1]), BF16),
        vmem((head_count, cells, width), BF16),
        vmem((head_count, cells, mine), BF16),
        vmem((head_count, cells, mine), BF16),
        vmem((cells, width), F32),
        vmem((cells, c_up.shape[1]), BF16),
        vmem((head_count, cells, width), BF16),
        vmem((head_count, cells, width), BF16),
        vmem((rows, C), BF16),
        vmem((C // 128, rows, 128), F32),
        dma((7,)), dma((2,)), dma((2,)), dma((4,)), dma((4, chips)), dma((4, region_count)), dma((4, chips)),
    ]
    scratch += [dma((head_count, chips)) for _ in range(4)]
    scratch += [dma((head_count,)) for _ in range(8)]
    return pl.pallas_call(
        functools.partial(kernel, region_count, head_count),
        out_shape=jax.ShapeDtypeStruct((rows, C), F32),
        in_specs=[pl.BlockSpec(memory_space=pltpu.SMEM)] * 2
        + [pl.BlockSpec(memory_space=pltpu.VMEM)] + [any_spec] * 11,
        out_specs=pl.BlockSpec(memory_space=pltpu.VMEM),
        scratch_shapes=scratch,
        compiler_params=pltpu.CompilerParams(
            collective_id=0, has_side_effects=True, vmem_limit_bytes=60 * 1024 * 1024
        ),
    )(shift, counts, tokens, *weights)


def solution(mesh):
    in_specs = (
        P(("region", "head"), None), P(), P("region"), P(), P(), P(), P(), P(),
        P("region", "head"), P("head", "region"), P("region", "head"), P("head", "region"), P(), P(),
    )
    out_specs = P(("region", "head"), None)
    run = functools.partial(body, mesh.shape["region"], mesh.shape["head"])
    return jax.shard_map(run, mesh=mesh, in_specs=in_specs, out_specs=out_specs, check_vma=False)
```

profile of v0, /device:TPU:8, one launch (start us, length us, event | category | flops | bytes accessed | tf_op | source)
XLA Modules:
  0.0 105.6 jit_solution(157955464198786629)
XLA Ops:
  0.7 102.6 %shard_map.136 = f32[576,512]{1,0:T(8,128)} custom-call(s32[1]{0:T(128)S(6)} %copy.16.shift, s32[4]{0:T(128)} %counts.1, f32[576,512]{1,0:T(8,128)} %tokens.1, bf16[512,1536]{1,0:T(8,128)(2,1)} %w_qkv.1, bf16[512,512]{1,0:T(8,128)(2,1)} %w_proj.1, bf16[512,2048]{1,0:T(8,128)(2,1)} %w_up.1, bf16[2048,512]{1,0:T(8,128)(2,1)} %w_down.1, ...), custom_call_target="tpu_custom_call" | custom-call | tf_op jit(solution)/shard_map/pallas_call | solution.py:423
  103.2 2.4 %copy.17 = f32[576,512]{1,0:T(8,128)} copy(f32[576,512]{1,0:T(8,128)} %shard_map.136) | data formatting | bytes 2359296
where the time goes:
time: 106 us
  Pallas kernels  103 us (97%)
  local copies, waits for them, and re-layouts  2.36 us (2%)
    pallas_call x1, Pallas kernels, body(): pl.pallas_call(functools.partial(kernel, region_count, head_count), out_s...  103 us
    unnamed x1, local copies, waits for them, and re-layouts  2.36 us

commit v1 on v0

v1 whole, which is shorter than its diff:
```python
import functools

import jax
import jax.numpy as jnp
from jax import lax
from jax.experimental import pallas as pl
from jax.experimental.pallas import tpu as pltpu
from jax.sharding import PartitionSpec as P

C = 512
HD = 64
HF = 8
WIN = 144
HEADS = HF
MESH = pl.DeviceIdType.MESH
F32 = jnp.float32
BF16 = jnp.bfloat16


def norm(values):
    average = jnp.mean(values, axis=-1, keepdims=True)
    centred = values - average
    spread = jnp.mean(centred * centred, axis=-1, keepdims=True)
    return centred * lax.rsqrt(spread + 1e-05)


def gelu(values):
    return 0.5 * values * (1.0 + lax.erf(values * (0.5**0.5)))


def dot(left, right):
    return jnp.dot(left, right, preferred_element_type=F32)


def flip(index, mask):
    result = index
    bit = 1
    while bit <= mask:
        if mask & bit:
            result = result + (1 - 2 * ((index // bit) % 2)) * bit
        bit *= 2
    return result


def attend(packed, head_count, count):
    blended = []
    for head in range(head_count):
        base = head * 3 * HD
        query = packed[:, base : base + HD]
        key = packed[:, base + HD : base + 2 * HD]
        value = packed[:, base + 2 * HD : base + 3 * HD]
        scores = lax.dot_general(
            query, key, (((1,), (1,)), ((), ())), preferred_element_type=F32
        ) * (HD**-0.5)
        if count is not None:
            place = lax.broadcasted_iota(jnp.int32, scores.shape, 1)
            scores = jnp.where(place < count, scores, -1e30)
        raised = jnp.exp(scores - jnp.max(scores, axis=-1, keepdims=True))
        weights = (raised / jnp.sum(raised, axis=-1, keepdims=True)).astype(BF16)
        blended.append(dot(weights, value).astype(BF16))
    return blended


def kernel(
    region_count, head_count,
    shift, counts, tokens, w_qkv, w_proj, w_up, w_down, w_merge,
    c_qkv, c_proj, c_up, c_down, w_expand, w_out,
    out,
    v_qkv, v_proj, v_up, v_down, v_merge, v_expand, v_out,
    g_qkv, g_proj, g_up, g_down,
    extended, rolled, packed, blended, fine, fine_bf, hidden, grouped,
    coarse, shared, c_packed, sent_blend, got_blend, mid, c_normed, c_hidden, term, parts, got_parts,
    wide, spread, lanes,
    local_sem, halo_send, halo_recv, own_sem, z_send, w_recv, p_send, q_send, q_recv, x_send, x_recv,
    a_send, a_recv, b_send, b_recv, m_send, m_recv, r_send, r_recv,
):
    region, head = lax.axis_index("region"), lax.axis_index("head")
    chips = region_count // 2
    chip, core = region // 2, region % 2
    rows = tokens.shape[0]
    blocks = rows // WIN
    flat = region * head_count + head
    total = region_count * head_count
    before, after = (flat + total - 1) % total, (flat + 1) % total
    before = (before // head_count, before % head_count)
    after = (after // head_count, after % head_count)
    partner = (chip * 2 + 1 - core, head)
    plane = [(region, flip(head, k)) for k in range(head_count)]
    ways = (1, -1)

    def line(way):
        return (((chip + way + chips) % chips) * 2 + core, head)

    barrier = pltpu.get_barrier_semaphore()
    greeted = [before, after, partner, line(1), line(-1)] + plane[1:]
    for device in greeted:
        pl.semaphore_signal(barrier, inc=1, device_id=device, device_id_type=MESH)

    QKV, PROJ, UP0, UP1, DOWN = range(5)
    half_up = c_up.shape[0] // 2
    shards = [c_qkv, c_proj, c_up.at[pl.ds(0, half_up)], c_up.at[pl.ds(half_up, half_up)], c_down]

    def slot(which, owner):
        if which == QKV:
            return g_qkv.at[pl.ds(owner * c_qkv.shape[0], c_qkv.shape[0])]
        if which == PROJ:
            return g_proj.at[head, owner]
        if which == UP0:
            return g_up.at[pl.ds(owner * c_up.shape[0], half_up)]
        if which == UP1:
            return g_up.at[pl.ds(owner * c_up.shape[0] + half_up, half_up)]
        return g_down.at[owner]

    own_shards = []
    for which in range(5):
        own_shards.append(pltpu.make_async_copy(shards[which], slot(which, region), own_sem.at[which]))
    own = []
    for at, (source, target) in enumerate(
        [(w_qkv, v_qkv), (w_proj, v_proj), (w_up, v_up), (w_down, v_down), (w_merge, v_merge),
         (w_expand, v_expand), (w_out, v_out)]
    ):
        own.append(pltpu.make_async_copy(source, target, local_sem.at[at]))
    own[0].start()
    for copy in own_shards + own[1:]:
        copy.start()

    def remote(source, target, send, recv, device):
        return pltpu.make_async_remote_copy(
            src_ref=source, dst_ref=target, send_sem=send, recv_sem=recv,
            device_id=device, device_id_type=MESH,
        )

    extended[WIN : WIN + rows, :] = norm(tokens[...]).astype(BF16)
    pl.semaphore_wait(barrier, len(greeted))

    halo_left = remote(extended.at[pl.ds(WIN, WIN)], extended.at[pl.ds(WIN + rows, WIN)],
                       halo_send.at[0], halo_recv.at[0], before)
    halo_right = remote(extended.at[pl.ds(rows, WIN)], extended.at[pl.ds(0, WIN)],
                        halo_send.at[1], halo_recv.at[1], after)
    halo_left.start()
    halo_right.start()

    def came(way, far):
        return (chip - way * far >= 0) & (chip - way * far < chips)

    def goes(way):
        return (chip + way >= 0) & (chip + way < chips)

    def owner_of(way, far):
        return ((chip - way * far + chips * chips) % chips) * 2 + core

    def hop(which, way, far):
        owner = owner_of(way, far)
        place = slot(which, owner)
        return remote(shards[which] if far == 0 else place, place,
                      z_send.at[which, (way < 0) * chips + far], w_recv.at[which, owner], line(way))

    def pass_over(which, owner, source=None):
        place = slot(which, owner)
        return remote(place if source is None else source, place, p_send.at[which, owner // 2], w_recv.at[which, owner], partner)

    def spread_proj(owner, at, source=None):
        for k in range(1, head_count):
            piece = g_proj.at[head, owner]
            remote(piece if source is None else source, piece, q_send.at[k, at], q_recv.at[k, owner // 2], plane[k]).start()

    def send_own(which):
        for way in ways:
            @pl.when(goes(way))
            def _():
                hop(which, way, 0).start()

    def arrive(which, way, far, forward):
        owner = owner_of(way, far)
        remote(slot(which, owner), slot(which, owner), p_send.at[which, owner // 2],
               w_recv.at[which, owner], line(way)).wait_recv()
        if forward:
            hop(which, way, far).start()
        pass_over(which, owner).start()
        if which == PROJ:
            spread_proj(owner, owner // 2)

    def forward(which, far):
        if far > chips - 2:
            return
        for way in ways:
            @pl.when(came(way, far) & goes(way))
            def _():
                arrive(which, way, far, True)

    def collect(which, fars):
        for far in fars:
            for way in ways:
                @pl.when(came(way, far) & jnp.logical_not(goes(way)))
                def _():
                    arrive(which, way, far, False)

    def take_one(which, owner):
        remote(slot(which, owner), slot(which, owner), p_send.at[which, owner // 2],
               w_recv.at[which, owner], partner).wait_recv()

    def take_over(which):
        for s in range(chips):
            take_one(which, ((chip + s) % chips) * 2 + 1 - core)

    fars = range(1, chips)

    for which in (PROJ, QKV, UP0):
        send_own(which)
    spread_proj(region, chip, shards[PROJ])
    for which in (PROJ, QKV, UP0, UP1, DOWN):
        pass_over(which, region, shards[which]).start()

    relay = head_count == 4

    def half_of(piece_of, h, i):
        whole = piece_of(h)
        half = whole.shape[1] // 2
        return whole.at[:, pl.ds(i * half, half)]

    def half_copy(piece_of, h, k, i, send, recv):
        piece = half_of(piece_of, h, i)
        return remote(piece, piece, send.at[k, i], recv.at[k, i], plane[k])

    def gather(piece_of, send, recv):
        copies = []
        for i in range(2):
            for k in range(1, 3 if relay else head_count):
                copy = half_copy(piece_of, head, k, i if k != 2 else 1 - i, send, recv)
                copy.start()
                copies.append(copy)
        return copies

    def far_half(piece_of, mask, i, send, recv, device):
        piece = half_of(piece_of, flip(head, mask), i)
        return remote(piece, piece, send.at[3, i], recv.at[3, i], device)

    def hand_on(piece_of, send, recv, copies):
        if not relay:
            return
        for i, (came_by, goes_by) in enumerate(((1, 2), (2, 1))):
            half_copy(piece_of, flip(head, came_by), came_by, i, send, recv).wait_recv()
            copy = far_half(piece_of, came_by, i, send, recv, plane[goes_by])
            copy.start()
            copies.append(copy)

    def arrived(piece_of, k, send, recv):
        for i in range(2):
            if relay and k == 3:
                far_half(piece_of, 3, i, send, recv, plane[2 - i]).wait_recv()
            elif not (relay and i == k - 1):
                half_copy(piece_of, flip(head, k), k, i, send, recv).wait_recv()

    offset = shift[0]
    at_row = lax.broadcasted_iota(jnp.int32, (WIN, 2 * WIN), 0)
    at_column = lax.broadcasted_iota(jnp.int32, (WIN, 2 * WIN), 1)
    forth = (at_column == at_row + offset).astype(F32).astype(BF16)
    back = (at_column == at_row + (WIN - offset)).astype(F32).astype(BF16)

    def place_of(j):
        return (j - 1) % (blocks + 1) if j > 0 else blocks - 1

    def roll_window(j):
        to = place_of(j) if j < blocks else blocks
        rolled[to * WIN : (to + 1) * WIN, :] = dot(
            forth, extended[j * WIN : (j + 2) * WIN, :]
        ).astype(BF16)

    def project_rows(first, last):
        def project(i, carry):
            at = pl.ds(pl.multiple_of(i * 256, 256), 256)
            packed[first:last, at] = dot(rolled[first:last, :], v_qkv[:, at]).astype(BF16)
            return carry

        lax.fori_loop(0, packed.shape[1] // 256, project, 0)

    def window(place, target):
        at = pl.ds(pl.multiple_of(place * WIN, WIN), WIN)
        to = pl.ds(pl.multiple_of(target * WIN, WIN), WIN)
        for half in range(2):
            width = packed.shape[1] // 2
            parts_of = attend(packed[at, half * width : (half + 1) * width], HEADS // 2, None)
            blended[to, half * (C // 2) : (half + 1) * (C // 2)] = jnp.concatenate(parts_of, axis=1)

    inner = blocks - 1

    def windows(first, last):
        def step(i, carry):
            window(i, jnp.where(i < inner, i + 1, (i - inner) * blocks))
            return carry

        lax.fori_loop(first, last, step, 0)

    for j in range(1, blocks):
        roll_window(j)
    own[0].wait()
    project_rows(0, inner * WIN)
    windows(0, inner)
    halo_left.wait()
    halo_right.wait()
    roll_window(0)
    roll_window(blocks)
    project_rows(inner * WIN, (blocks + 1) * WIN)
    forward(PROJ, 1)
    forward(QKV, 1)
    windows(inner, blocks + 1)

    collect(PROJ, fars[:1])
    for far in fars[1:]:
        forward(PROJ, far)
    own[1].wait()
    for j in range(blocks):
        at = slice(j * WIN, (j + 1) * WIN)
        rolled[at, :] = dot(back, blended[j * WIN : (j + 2) * WIN, :]).astype(BF16)
    fine[...] = tokens[...] + dot(rolled[:rows, :], v_proj[...])
    rolled[:rows, :] = norm(fine[...]).astype(BF16)

    own[2].wait()

    def fine_hidden(i, carry):
        at = pl.ds(pl.multiple_of(i * 256, 256), 256)
        hidden[:, at] = gelu(dot(rolled[:rows, :], v_up[:, at])).astype(BF16)
        return carry

    chunks = hidden.shape[1] // 256
    lax.fori_loop(0, chunks, fine_hidden, 0)
    collect(PROJ, fars[1:2])
    for far in fars[1:]:
        forward(QKV, far)
    send_own(UP1)
    own[3].wait()

    def fine_sum(i, carry):
        at = pl.ds(pl.multiple_of(i * 256, 256), 256)
        fine[:, at] += dot(hidden[...], v_down[:, at])
        return carry

    lax.fori_loop(0, C // 256, fine_sum, 0)
    collect(PROJ, fars[2:])
    forward(UP0, 1)

    group = w_merge.shape[0] // C
    cells = rows // group
    own[4].wait()
    members = []
    for c in range(C // 128):
        lanes[c] = fine[:, c * 128 : (c + 1) * 128]
    for k in range(group):
        pieces = [lanes[c, pl.ds(k, cells, stride=group), :] for c in range(C // 128)]
        member = jnp.concatenate(pieces, axis=1)
        fine_bf[k * cells : (k + 1) * cells, :] = member.astype(BF16)
        members.append(member)
    merged = jnp.concatenate(members, axis=1)
    grouped[...] = norm(merged).astype(BF16)
    width = coarse.shape[1]

    def merge(i, carry):
        at = pl.ds(pl.multiple_of(i * 256, 256), 256)
        coarse[:, at] = dot(grouped[...], v_merge[:, at])
        return carry

    lax.fori_loop(0, width // 256, merge, 0)

    def shared_of(h):
        return shared.at[h]

    shared[head] = norm(coarse[...]).astype(BF16)
    gathers = gather(shared_of, a_send, a_recv)
    own_shards[QKV].wait()
    collect(QKV, fars)
    take_over(QKV)

    blends = []
    heads_here = g_qkv.shape[1] // (3 * HD)
    for k in range(head_count):
        target = plane[k][1]
        if k > 0:
            arrived(shared_of, k, a_send, a_recv)
        c_packed[...] = dot(shared[target], g_qkv[...]).astype(BF16)
        parts_of = attend(c_packed[...], heads_here, counts[target])
        if k == 0:
            got_blend[head] = jnp.concatenate(parts_of, axis=1)
            hand_on(shared_of, a_send, a_recv, gathers)
        else:
            sent_blend[k] = jnp.concatenate(parts_of, axis=1)
            copy = remote(sent_blend.at[k], got_blend.at[head], b_send.at[k], b_recv.at[k], plane[k])
            copy.start()
            blends.append(copy)
        if k == min(1, head_count - 1):
            forward(UP1, 1)
        if k == min(2, head_count - 1):
            for which in (UP0, UP1):
                for far in fars[1:]:
                    forward(which, far)
            send_own(DOWN)
    for s in range(chips):
        owner = ((chip + s) % chips) * 2 + core
        for k in range(1, head_count):
            piece = g_proj.at[plane[k][1], owner]
            remote(piece, piece, q_send.at[k, s], q_recv.at[k, owner // 2], plane[k]).wait_recv()
            remote(piece, piece, x_send.at[k, s], x_recv.at[k, owner // 2], partner).start()
    own_shards[PROJ].wait()
    take_over(PROJ)
    for s in range(chips):
        owner = ((chip + s) % chips) * 2 + 1 - core
        for k in range(1, head_count):
            piece = g_proj.at[plane[k][1], owner]
            remote(piece, piece, x_send.at[k, s], x_recv.at[k, owner // 2], partner).wait_recv()
    for copy in blends:
        copy.wait_recv()
    for r in range(region_count):
        w = g_proj.shape[3]
        total_of = dot(got_blend[0], g_proj[0, r])
        for h in range(1, head_count):
            total_of += dot(got_blend[h], g_proj[h, r])
        mid[:, r * w : (r + 1) * w] = coarse[:, r * w : (r + 1) * w] + total_of

    def row_block(h):
        return pl.ds(pl.multiple_of(h * cells, cells), cells)

    def normed_of(h):
        return c_normed.at[row_block(h)]

    c_normed[row_block(head), :] = norm(mid[...]).astype(BF16)
    seconds = gather(normed_of, m_send, m_recv)
    forward(DOWN, 1)
    own[5].wait()
    own[6].wait()
    for c in range(C // 256):
        at = slice(c * 256, (c + 1) * 256)
        fine[:, at] = dot(fine_bf[...], v_out[:C, at])
    hand_on(normed_of, m_send, m_recv, seconds)
    for which in (UP0, UP1):
        own_shards[which].wait()
        collect(which, fars)
        take_over(which)
    for k in range(1, head_count):
        arrived(normed_of, k, m_send, m_recv)
    for far in fars[1:]:
        forward(DOWN, far)

    def coarse_hidden(i, carry):
        at = pl.ds(pl.multiple_of(i * 256, 256), 256)
        c_hidden[:, at] = gelu(dot(c_normed[...], g_up[:, at])).astype(BF16)
        return carry

    lax.fori_loop(0, c_hidden.shape[1] // 256, coarse_hidden, 0)

    turn = 1 - 2 * (chip // ((chips + 1) // 2))
    w = g_down.shape[2]
    pair = 2 * w

    def chip_at(s):
        return (chip + turn * s + chips * chips) % chips

    own_shards[DOWN].wait()
    returns = []
    for s in range(chips):
        holder = chip_at(s)
        columns = pl.ds(pl.multiple_of(holder * pair, pair), pair)
        if s > 0:
            for far in fars:
                for way in ways:
                    @pl.when(came(way, far) & jnp.logical_not(goes(way)) & (owner_of(way, far) // 2 == holder))
                    def _():
                        arrive(DOWN, way, far, False)
        take_one(DOWN, holder * 2 + 1 - core)
        weights = jnp.concatenate([g_down[holder * 2], g_down[holder * 2 + 1]], axis=1)
        term[...] = dot(c_hidden[...], weights)
        mid[:, columns] += term[row_block(head), :]
        for k in range(1, head_count):
            parts[k, :, columns] = term[row_block(plane[k][1]), :].astype(BF16)
            copy = remote(parts.at[k, :, columns], got_parts.at[k, :, columns],
                          r_send.at[k, s], r_recv.at[k, s], plane[k])
            copy.start()
            returns.append(copy)
    for s in range(chips):
        columns = pl.ds(pl.multiple_of(chip_at(s) * pair, pair), pair)
        for k in range(1, head_count):
            returns[s * (head_count - 1) + k - 1].wait_recv()
        result = mid[:, columns]
        for k in range(1, head_count):
            result += got_parts[k, :, columns].astype(F32)
        result = result.astype(BF16)
        for k in range(group):
            at = slice(k * C, (k + 1) * C)
            piece = dot(result, v_expand[columns, at])
            if s > 0:
                piece += wide[:, at]
            if s < chips - 1:
                wide[:, at] = piece
            else:
                spread[k * cells : (k + 1) * cells, :] = piece.astype(BF16)
    for c in range(C // 128):
        at = slice(c * 128, (c + 1) * 128)
        value = fine[:, at] + dot(spread[...], v_out[C:, at])
        for k in range(group):
            lanes[c, pl.ds(k, cells, stride=group), :] = value[k * cells : (k + 1) * cells, :]
        out[:, at] = lanes[c]

    for copy in gathers + blends + seconds + returns:
        copy.wait_send()
    for which in range(5):
        for way in ways:
            @pl.when(goes(way))
            def _():
                hop(which, way, 0).wait_send()
            for far in fars[:-1]:
                @pl.when(came(way, far) & goes(way))
                def _():
                    hop(which, way, far).wait_send()
        for s in range(chips):
            pass_over(which, ((chip + s) % chips) * 2 + core).wait_send()
    for s in range(chips):
        owner = ((chip + s) % chips) * 2 + core
        for k in range(1, head_count):
            piece = g_proj.at[head, owner]
            remote(piece, piece, q_send.at[k, owner // 2], q_recv.at[k, owner // 2], plane[k]).wait_send()
            piece = g_proj.at[plane[k][1], owner]
            remote(piece, piece, x_send.at[k, s], x_recv.at[k, owner // 2], partner).wait_send()


def body(region_count, head_count, tokens, shift, counts, *weights):
    rows = tokens.shape[0]
    w_qkv, w_proj, w_up, w_down, w_merge, c_qkv, c_proj, c_up, c_down, w_expand, w_out = weights
    width = w_merge.shape[1]
    group = w_merge.shape[0] // C
    cells = rows // group
    vmem = pltpu.VMEM
    any_spec = pl.BlockSpec(memory_space=pl.ANY)
    dma = pltpu.SemaphoreType.DMA
    chips = region_count // 2
    mine = c_proj.shape[0]
    scratch = [vmem(w.shape, BF16) for w in (w_qkv, w_proj, w_up, w_down, w_merge, w_expand, w_out)]
    scratch += [
        vmem((width, c_qkv.shape[1]), BF16),
        vmem((head_count, region_count) + c_proj.shape, BF16),
        vmem((width, c_up.shape[1]), BF16),
        vmem((region_count,) + c_down.shape, BF16),
        vmem((rows + 2 * WIN, C), BF16),
        vmem((rows + WIN, C), BF16),
        vmem((rows + WIN, w_qkv.shape[1]), BF16),
        vmem((rows + WIN, C), BF16),
        vmem((rows, C), F32),
        vmem((rows, C), BF16),
        vmem((rows, w_up.shape[1]), BF16),
        vmem((cells, group * C), BF16),
        vmem((cells, width), F32),
        vmem((head_count, cells, width), BF16),
        vmem((cells, c_qkv.shape[1]), BF16),
        vmem((head_count, cells, mine), BF16),
        vmem((head_count, cells, mine), BF16),
        vmem((cells, width), F32),
        vmem((head_count * cells, width), BF16),
        vmem((head_count * cells, c_up.shape[1]), BF16),
        vmem((head_count * cells, 2 * c_down.shape[1]), F32),
        vmem((head_count, cells, width), BF16),
        vmem((head_count, cells, width), BF16),
        vmem((cells, group * C), F32),
        vmem((rows, C), BF16),
        vmem((C // 128, rows, 128), F32),
        dma((7,)), dma((2,)), dma((2,)), dma((5,)), dma((5, 2 * chips)), dma((5, region_count)), dma((5, chips)),
    ]
    scratch += [dma((head_count, chips)) for _ in range(4)]
    scratch += [
        dma((head_count, 2)), dma((head_count, 2)), dma((head_count,)), dma((head_count,)), dma((head_count, 2)),
        dma((head_count, 2)), dma((head_count, chips)), dma((head_count, chips)),
    ]
    return pl.pallas_call(
        functools.partial(kernel, region_count, head_count),
        out_shape=jax.ShapeDtypeStruct((rows, C), F32),
        in_specs=[pl.BlockSpec(memory_space=pltpu.SMEM)] * 2
        + [pl.BlockSpec(memory_space=pltpu.VMEM)] + [any_spec] * 11,
        out_specs=pl.BlockSpec(memory_space=pltpu.VMEM),
        scratch_shapes=scratch,
        compiler_params=pltpu.CompilerParams(
            collective_id=0, has_side_effects=True, vmem_limit_bytes=60 * 1024 * 1024
        ),
    )(shift, counts, tokens, *weights)


def solution(mesh):
    in_specs = (
        P(("region", "head"), None), P(), P("region"), P(), P(), P(), P(), P(),
        P("region", "head"), P("head", "region"), P("region", "head"), P("head", "region"), P(), P(),
    )
    out_specs = P(("region", "head"), None)
    run = functools.partial(body, mesh.shape["region"], mesh.shape["head"])
    return jax.shard_map(run, mesh=mesh, in_specs=in_specs, out_specs=out_specs, check_vma=False)
```

time: 106 us -> 84.2 us (0.79)
  the two profiles are of different devices: /device:TPU:8 before, /device:TPU:0 now
where the time goes in v1:
time: 84.2 us; the launch traced here: 84.1 us
  Pallas kernels  81 us (96%)
  local copies, waits for them, and re-layouts  2.36 us (3%)
    pallas_call x1, Pallas kernels, body(): pl.pallas_call(functools.partial(kernel, region_count, head_count), out_s...  81 us
    unnamed x1, local copies, waits for them, and re-layouts  2.36 us

profile of v1, /device:TPU:0, one launch (start us, length us, event | category | flops | bytes accessed | tf_op | source)
XLA Modules:
  0.0 84.1 jit_solution(16835708844157839524)
XLA Ops:
  0.7 81.0 %shard_map.136 = f32[576,512]{1,0:T(8,128)} custom-call(s32[1]{0:T(128)S(6)} %copy.16.shift, s32[4]{0:T(128)} %counts.1, f32[576,512]{1,0:T(8,128)} %tokens.1, bf16[512,1536]{1,0:T(8,128)(2,1)} %w_qkv.1, bf16[512,512]{1,0:T(8,128)(2,1)} %w_proj.1, bf16[512,2048]{1,0:T(8,128)(2,1)} %w_up.1, bf16[2048,512]{1,0:T(8,128)(2,1)} %w_down.1, ...), custom_call_target="tpu_custom_call" | custom-call | tf_op jit(solution)/shard_map/pallas_call | solution.py:569
  81.7 2.4 %copy.17 = f32[576,512]{1,0:T(8,128)} copy(f32[576,512]{1,0:T(8,128)} %shard_map.136) | data formatting | bytes 2359296

commit v2 on v1

--- a/solution.py
+++ b/solution.py
@@ -15,6 +15,7 @@
 MESH = pl.DeviceIdType.MESH
 F32 = jnp.float32
 BF16 = jnp.bfloat16
+LOG2E = 1.4426950408889634
 
 
 def norm(values):
@@ -42,7 +43,8 @@
     return result
 
 
-def attend(packed, head_count, count):
+def attend(packed, head_count, visible):
+    scale = HD**-0.5
     blended = []
     for head in range(head_count):
         base = head * 3 * HD
@@ -50,14 +52,16 @@
         key = packed[:, base + HD : base + 2 * HD]
         value = packed[:, base + 2 * HD : base + 3 * HD]
         scores = lax.dot_general(
-            query, key, (((1,), (1,)), ((), ())), preferred_element_type=F32
-        ) * (HD**-0.5)
-        if count is not None:
-            place = lax.broadcasted_iota(jnp.int32, scores.shape, 1)
-            scores = jnp.where(place < count, scores, -1e30)
-        raised = jnp.exp(scores - jnp.max(scores, axis=-1, keepdims=True))
-        weights = (raised / jnp.sum(raised, axis=-1, keepdims=True)).astype(BF16)
-        blended.append(dot(weights, value).astype(BF16))
+            key, query, (((1,), (1,)), ((), ())), preferred_element_type=F32
+        )
+        if visible is not None:
+            scores = jnp.where(visible, scores, -1e30 / scale)
+        raised = jnp.exp2((scores - jnp.max(scores, axis=0, keepdims=True)) * (scale * LOG2E))
+        weights = (raised * (1.0 / jnp.sum(raised, axis=0, keepdims=True))).astype(BF16)
+        mixed = lax.dot_general(
+            weights, value, (((0,), (0,)), ((), ())), preferred_element_type=F32
+        )
+        blended.append(mixed.astype(BF16))
     return blended
 
 
@@ -68,8 +72,8 @@
     out,
     v_qkv, v_proj, v_up, v_down, v_merge, v_expand, v_out,
     g_qkv, g_proj, g_up, g_down,
-    extended, rolled, packed, blended, fine, fine_bf, hidden, grouped,
-    coarse, shared, c_packed, sent_blend, got_blend, mid, c_normed, c_hidden, term, parts, got_parts,
+    extended, rolled, packed, blended, fine, fine_bf, hidden,
+    coarse, shared, sent_blend, got_blend, mid, c_normed, c_hidden, parts, got_parts,
     wide, spread, lanes,
     local_sem, halo_send, halo_recv, own_sem, z_send, w_recv, p_send, q_send, q_recv, x_send, x_recv,
     a_send, a_recv, b_send, b_recv, m_send, m_recv, r_send, r_recv,
@@ -120,8 +124,7 @@
          (w_expand, v_expand), (w_out, v_out)]
     ):
         own.append(pltpu.make_async_copy(source, target, local_sem.at[at]))
-    own[0].start()
-    for copy in own_shards + own[1:]:
+    for copy in (own_shards[0], own_shards[1], own[0], own[1]):
         copy.start()
 
     def remote(source, target, send, recv, device):
@@ -152,17 +155,24 @@
     def hop(which, way, far):
         owner = owner_of(way, far)
         place = slot(which, owner)
-        return remote(shards[which] if far == 0 else place, place,
+        return remote(place, place,
                       z_send.at[which, (way < 0) * chips + far], w_recv.at[which, owner], line(way))
 
-    def pass_over(which, owner, source=None):
+    def pass_over(which, owner):
         place = slot(which, owner)
-        return remote(place if source is None else source, place, p_send.at[which, owner // 2], w_recv.at[which, owner], partner)
-
-    def spread_proj(owner, at, source=None):
+        return remote(place, place, p_send.at[which, owner // 2], w_recv.at[which, owner], partner)
+
+    def chip_at(s):
+        if chips != 4:
+            return (chip + s) % chips
+        side = chip // 2
+        return (chip, flip(chip, 1), 2 * (1 - side) + side, 2 * (1 - side) + 1 - side)[s]
+
+    def spread_proj(s):
+        owner = chip_at(s) * 2 + core
         for k in range(1, head_count):
             piece = g_proj.at[head, owner]
-            remote(piece if source is None else source, piece, q_send.at[k, at], q_recv.at[k, owner // 2], plane[k]).start()
+            remote(piece, piece, q_send.at[k, owner // 2], q_recv.at[k, owner // 2], plane[k]).start()
 
     def send_own(which):
         for way in ways:
@@ -177,8 +187,6 @@
         if forward:
             hop(which, way, far).start()
         pass_over(which, owner).start()
-        if which == PROJ:
-            spread_proj(owner, owner // 2)
 
     def forward(which, far):
         if far > chips - 2:
@@ -205,11 +213,12 @@
 
     fars = range(1, chips)
 
-    for which in (PROJ, QKV, UP0):
+    for which in (QKV, PROJ):
+        own_shards[which].wait()
         send_own(which)
-    spread_proj(region, chip, shards[PROJ])
-    for which in (PROJ, QKV, UP0, UP1, DOWN):
-        pass_over(which, region, shards[which]).start()
+        pass_over(which, region).start()
+    for copy in own[2:5] + own_shards[2:] + own[5:]:
+        copy.start()
 
     relay = head_count == 4
 
@@ -267,139 +276,149 @@
         ).astype(BF16)
 
     def project_rows(first, last):
-        def project(i, carry):
-            at = pl.ds(pl.multiple_of(i * 256, 256), 256)
-            packed[first:last, at] = dot(rolled[first:last, :], v_qkv[:, at]).astype(BF16)
-            return carry
-
-        lax.fori_loop(0, packed.shape[1] // 256, project, 0)
-
-    def window(place, target):
-        at = pl.ds(pl.multiple_of(place * WIN, WIN), WIN)
-        to = pl.ds(pl.multiple_of(target * WIN, WIN), WIN)
-        for half in range(2):
-            width = packed.shape[1] // 2
-            parts_of = attend(packed[at, half * width : (half + 1) * width], HEADS // 2, None)
-            blended[to, half * (C // 2) : (half + 1) * (C // 2)] = jnp.concatenate(parts_of, axis=1)
+        packed[first:last, :] = dot(rolled[first:last, :], v_qkv[...]).astype(BF16)
 
     inner = blocks - 1
 
     def windows(first, last):
-        def step(i, carry):
-            window(i, jnp.where(i < inner, i + 1, (i - inner) * blocks))
-            return carry
-
-        lax.fori_loop(first, last, step, 0)
+        for place in range(first, last):
+            target = place + 1 if place < inner else (place - inner) * blocks
+            at = slice(place * WIN, (place + 1) * WIN)
+            blended[target * WIN : (target + 1) * WIN, :] = jnp.concatenate(
+                attend(packed[at, :], HEADS, None), axis=1
+            )
+
+    group = w_merge.shape[0] // C
+    cells = rows // group
+    width = coarse.shape[1]
+    near, edge = list(range(1, blocks - 1)), [0, blocks - 1]
+    order = near + edge
+    spans = [(0, len(near) * WIN), (len(near) * WIN, rows)]
+
+    def fine_chunk(index):
+        first, last = spans[index]
+        members_of = (near, edge)[index]
+        for p, j in enumerate(members_of):
+            rolled[first + p * WIN : first + (p + 1) * WIN, :] = dot(
+                back, blended[j * WIN : (j + 2) * WIN, :]
+            ).astype(BF16)
+        own[1].wait() if index == 0 else None
+        attended = dot(rolled[first:last, :], v_proj[...])
+        for p, j in enumerate(members_of):
+            fine[first + p * WIN : first + (p + 1) * WIN, :] = (
+                tokens[j * WIN : (j + 1) * WIN, :] + attended[p * WIN : (p + 1) * WIN, :]
+            )
+        rolled[first:last, :] = norm(fine[first:last, :]).astype(BF16)
+        own[2].wait() if index == 0 else None
+        hidden[first:last, :] = gelu(dot(rolled[first:last, :], v_up[...])).astype(BF16)
+        own[3].wait() if index == 0 else None
+        fine[first:last, :] += dot(hidden[first:last, :], v_down[...])
+
+    def merge_chunk(index):
+        first, last = spans[index]
+        low, high = first // group, last // group
+        for c in range(C // 128):
+            lanes[c, first:last, :] = fine[first:last, c * 128 : (c + 1) * 128]
+        members = []
+        for k in range(group):
+            pieces = [lanes[c, pl.ds(first + k, high - low, stride=group), :] for c in range(C // 128)]
+            members.append(jnp.concatenate(pieces, axis=1))
+        fine_bf[first:last, :] = jnp.concatenate(members, axis=0).astype(BF16)
+        own[4].wait() if index == 0 else None
+        coarse[low:high, :] = dot(norm(jnp.concatenate(members, axis=1)).astype(BF16), v_merge[...])
+        shared[index, head] = norm(coarse[low:high, :]).astype(BF16)
+
+    def shared_of(index):
+        return lambda h: shared.at[index, h]
 
     for j in range(1, blocks):
         roll_window(j)
     own[0].wait()
     project_rows(0, inner * WIN)
     windows(0, inner)
+    fine_chunk(0)
+    forward(QKV, 1)
+    merge_chunk(0)
+    gathers = gather(shared_of(0), a_send.at[0], a_recv.at[0])
     halo_left.wait()
     halo_right.wait()
+    forward(PROJ, 1)
+    collect(PROJ, fars[:1])
+    for s in range(min(2, chips)):
+        spread_proj(s)
     roll_window(0)
     roll_window(blocks)
     project_rows(inner * WIN, (blocks + 1) * WIN)
-    forward(PROJ, 1)
-    forward(QKV, 1)
     windows(inner, blocks + 1)
-
-    collect(PROJ, fars[:1])
+    for far in fars[1:]:
+        forward(QKV, far)
+    for which in (UP0, UP1, DOWN):
+        own_shards[which].wait()
+        pass_over(which, region).start()
+    send_own(UP0)
+    hand_on(shared_of(0), a_send.at[0], a_recv.at[0], gathers)
+    fine_chunk(1)
     for far in fars[1:]:
         forward(PROJ, far)
-    own[1].wait()
-    for j in range(blocks):
-        at = slice(j * WIN, (j + 1) * WIN)
-        rolled[at, :] = dot(back, blended[j * WIN : (j + 2) * WIN, :]).astype(BF16)
-    fine[...] = tokens[...] + dot(rolled[:rows, :], v_proj[...])
-    rolled[:rows, :] = norm(fine[...]).astype(BF16)
-
-    own[2].wait()
-
-    def fine_hidden(i, carry):
-        at = pl.ds(pl.multiple_of(i * 256, 256), 256)
-        hidden[:, at] = gelu(dot(rolled[:rows, :], v_up[:, at])).astype(BF16)
-        return carry
-
-    chunks = hidden.shape[1] // 256
-    lax.fori_loop(0, chunks, fine_hidden, 0)
-    collect(PROJ, fars[1:2])
-    for far in fars[1:]:
-        forward(QKV, far)
+    merge_chunk(1)
+    gathers += gather(shared_of(1), a_send.at[1], a_recv.at[1])
     send_own(UP1)
-    own[3].wait()
-
-    def fine_sum(i, carry):
-        at = pl.ds(pl.multiple_of(i * 256, 256), 256)
-        fine[:, at] += dot(hidden[...], v_down[:, at])
-        return carry
-
-    lax.fori_loop(0, C // 256, fine_sum, 0)
-    collect(PROJ, fars[2:])
-    forward(UP0, 1)
-
-    group = w_merge.shape[0] // C
-    cells = rows // group
-    own[4].wait()
-    members = []
-    for c in range(C // 128):
-        lanes[c] = fine[:, c * 128 : (c + 1) * 128]
-    for k in range(group):
-        pieces = [lanes[c, pl.ds(k, cells, stride=group), :] for c in range(C // 128)]
-        member = jnp.concatenate(pieces, axis=1)
-        fine_bf[k * cells : (k + 1) * cells, :] = member.astype(BF16)
-        members.append(member)
-    merged = jnp.concatenate(members, axis=1)
-    grouped[...] = norm(merged).astype(BF16)
-    width = coarse.shape[1]
-
-    def merge(i, carry):
-        at = pl.ds(pl.multiple_of(i * 256, 256), 256)
-        coarse[:, at] = dot(grouped[...], v_merge[:, at])
-        return carry
-
-    lax.fori_loop(0, width // 256, merge, 0)
-
-    def shared_of(h):
-        return shared.at[h]
-
-    shared[head] = norm(coarse[...]).astype(BF16)
-    gathers = gather(shared_of, a_send, a_recv)
-    own_shards[QKV].wait()
     collect(QKV, fars)
     take_over(QKV)
 
+    at_key = lax.broadcasted_iota(jnp.int32, (cells, cells), 0)
+    block_cells = WIN // group
+    inside = len(near) * block_cells
+    place = jnp.where(
+        at_key < inside, at_key + block_cells, jnp.where(at_key < inside + block_cells, at_key - inside, at_key)
+    )
+
     blends = []
     heads_here = g_qkv.shape[1] // (3 * HD)
-    for k in range(head_count):
-        target = plane[k][1]
-        if k > 0:
-            arrived(shared_of, k, a_send, a_recv)
-        c_packed[...] = dot(shared[target], g_qkv[...]).astype(BF16)
-        parts_of = attend(c_packed[...], heads_here, counts[target])
-        if k == 0:
-            got_blend[head] = jnp.concatenate(parts_of, axis=1)
-            hand_on(shared_of, a_send, a_recv, gathers)
-        else:
-            sent_blend[k] = jnp.concatenate(parts_of, axis=1)
+
+    def coarse_attention(ks):
+        packed_of = [
+            jnp.concatenate(
+                [dot(shared[index, plane[k][1]], g_qkv[...]) for index in range(2)], axis=0
+            ).astype(BF16)
+            for k in ks
+        ]
+        for k, its in zip(ks, packed_of):
+            parts_of = attend(its, heads_here, place < counts[plane[k][1]])
+            if k == 0:
+                got_blend[head] = jnp.concatenate(parts_of, axis=1)
+            else:
+                sent_blend[k] = jnp.concatenate(parts_of, axis=1)
+
+    forward(UP0, 1)
+    coarse_attention([0])
+    hand_on(shared_of(1), a_send.at[1], a_recv.at[1], gathers)
+    collect(PROJ, fars[1:])
+    for s in range(2, chips):
+        spread_proj(s)
+    forward(UP1, 1)
+    for far in fars[1:]:
+        forward(UP0, far)
+    send_own(DOWN)
+    for ks in [range(1, min(3, head_count)), range(3, head_count)]:
+        for k in ks:
+            for index in range(2):
+                arrived(shared_of(index), k, a_send.at[index], a_recv.at[index])
+        coarse_attention(ks)
+        for k in ks:
             copy = remote(sent_blend.at[k], got_blend.at[head], b_send.at[k], b_recv.at[k], plane[k])
             copy.start()
             blends.append(copy)
-        if k == min(1, head_count - 1):
-            forward(UP1, 1)
-        if k == min(2, head_count - 1):
-            for which in (UP0, UP1):
-                for far in fars[1:]:
-                    forward(which, far)
-            send_own(DOWN)
+        if 1 in ks:
+            for far in fars[1:]:
+                forward(UP1, far)
+    forward(DOWN, 1)
     for s in range(chips):
         owner = ((chip + s) % chips) * 2 + core
         for k in range(1, head_count):
             piece = g_proj.at[plane[k][1], owner]
             remote(piece, piece, q_send.at[k, s], q_recv.at[k, owner // 2], plane[k]).wait_recv()
             remote(piece, piece, x_send.at[k, s], x_recv.at[k, owner // 2], partner).start()
-    own_shards[PROJ].wait()
     take_over(PROJ)
     for s in range(chips):
         owner = ((chip + s) % chips) * 2 + 1 - core
@@ -423,7 +442,8 @@
 
     c_normed[row_block(head), :] = norm(mid[...]).astype(BF16)
     seconds = gather(normed_of, m_send, m_recv)
-    forward(DOWN, 1)
+    for far in fars[1:]:
+        forward(DOWN, far)
     own[5].wait()
     own[6].wait()
     for c in range(C // 256):
@@ -431,33 +451,17 @@
         fine[:, at] = dot(fine_bf[...], v_out[:C, at])
     hand_on(normed_of, m_send, m_recv, seconds)
     for which in (UP0, UP1):
-        own_shards[which].wait()
         collect(which, fars)
         take_over(which)
-    for k in range(1, head_count):
-        arrived(normed_of, k, m_send, m_recv)
-    for far in fars[1:]:
-        forward(DOWN, far)
-
-    def coarse_hidden(i, carry):
-        at = pl.ds(pl.multiple_of(i * 256, 256), 256)
-        c_hidden[:, at] = gelu(dot(c_normed[...], g_up[:, at])).astype(BF16)
-        return carry
-
-    lax.fori_loop(0, c_hidden.shape[1] // 256, coarse_hidden, 0)
-
-    turn = 1 - 2 * (chip // ((chips + 1) // 2))
     w = g_down.shape[2]
     pair = 2 * w
-
-    def chip_at(s):
-        return (chip + turn * s + chips * chips) % chips
-
-    own_shards[DOWN].wait()
     returns = []
-    for s in range(chips):
+
+    def columns_of(s):
+        return pl.ds(pl.multiple_of(chip_at(s) * pair, pair), pair)
+
+    def down_ready(s):
         holder = chip_at(s)
-        columns = pl.ds(pl.multiple_of(holder * pair, pair), pair)
         if s > 0:
             for far in fars:
                 for way in ways:
@@ -465,19 +469,46 @@
                     def _():
                         arrive(DOWN, way, far, False)
         take_one(DOWN, holder * 2 + 1 - core)
+
+    def down(k, s):
+        holder = chip_at(s)
         weights = jnp.concatenate([g_down[holder * 2], g_down[holder * 2 + 1]], axis=1)
-        term[...] = dot(c_hidden[...], weights)
-        mid[:, columns] += term[row_block(head), :]
+        product = dot(c_hidden[row_block(plane[k][1]), :], weights)
+        if k == 0:
+            mid[:, columns_of(s)] += product
+        else:
+            parts[k, :, columns_of(s)] = product.astype(BF16)
+
+    def send_back(k, s):
+        copy = remote(parts.at[k, :, columns_of(s)], got_parts.at[k, :, columns_of(s)],
+                      r_send.at[k, s], r_recv.at[k, s], plane[k])
+        copy.start()
+        returns.append(copy)
+
+    early = min(2, chips)
+    for k in range(head_count):
+        at = row_block(plane[k][1])
+        if k > 0:
+            arrived(normed_of, k, m_send, m_recv)
+        c_hidden[at, :] = gelu(dot(c_normed[at, :], g_up[...])).astype(BF16)
+        for s in range(early):
+            if k == 0:
+                down_ready(s)
+        for s in range(early):
+            down(k, s)
+            if k > 0:
+                send_back(k, s)
+    for s in range(early, chips):
+        down_ready(s)
+        for k in [*range(1, head_count), 0]:
+            down(k, s)
+            if k > 0:
+                send_back(k, s)
+    for s in range(chips):
+        columns = columns_of(s)
         for k in range(1, head_count):
-            parts[k, :, columns] = term[row_block(plane[k][1]), :].astype(BF16)
-            copy = remote(parts.at[k, :, columns], got_parts.at[k, :, columns],
-                          r_send.at[k, s], r_recv.at[k, s], plane[k])
-            copy.start()
-            returns.append(copy)
-    for s in range(chips):
-        columns = pl.ds(pl.multiple_of(chip_at(s) * pair, pair), pair)
-        for k in range(1, head_count):
-            returns[s * (head_count - 1) + k - 1].wait_recv()
+            remote(parts.at[k, :, columns], got_parts.at[k, :, columns],
+                   r_send.at[k, s], r_recv.at[k, s], plane[k]).wait_recv()
         result = mid[:, columns]
         for k in range(1, head_count):
             result += got_parts[k, :, columns].astype(F32)
@@ -487,16 +518,21 @@
             piece = dot(result, v_expand[columns, at])
             if s > 0:
                 piece += wide[:, at]
-            if s < chips - 1:
-                wide[:, at] = piece
-            else:
-                spread[k * cells : (k + 1) * cells, :] = piece.astype(BF16)
+            wide[:, at] = piece
+    for first, last in spans:
+        low, high = first // group, last // group
+        spread[first:last, :] = jnp.concatenate(
+            [wide[low:high, k * C : (k + 1) * C] for k in range(group)], axis=0
+        ).astype(BF16)
     for c in range(C // 128):
         at = slice(c * 128, (c + 1) * 128)
         value = fine[:, at] + dot(spread[...], v_out[C:, at])
-        for k in range(group):
-            lanes[c, pl.ds(k, cells, stride=group), :] = value[k * cells : (k + 1) * cells, :]
-        out[:, at] = lanes[c]
+        for first, last in spans:
+            count = (last - first) // group
+            for k in range(group):
+                lanes[c, pl.ds(first + k, count, stride=group), :] = value[first + k * count : first + (k + 1) * count, :]
+        for p, j in enumerate(order):
+            out[j * WIN : (j + 1) * WIN, at] = lanes[c, p * WIN : (p + 1) * WIN, :]
 
     for copy in gathers + blends + seconds + returns:
         copy.wait_send()
@@ -544,16 +580,13 @@
         vmem((rows, C), F32),
         vmem((rows, C), BF16),
         vmem((rows, w_up.shape[1]), BF16),
-        vmem((cells, group * C), BF16),
         vmem((cells, width), F32),
-        vmem((head_count, cells, width), BF16),
-        vmem((cells, c_qkv.shape[1]), BF16),
+        vmem((2, head_count, cells // 2, width), BF16),
         vmem((head_count, cells, mine), BF16),
         vmem((head_count, cells, mine), BF16),
         vmem((cells, width), F32),
         vmem((head_count * cells, width), BF16),
         vmem((head_count * cells, c_up.shape[1]), BF16),
-        vmem((head_count * cells, 2 * c_down.shape[1]), F32),
         vmem((head_count, cells, width), BF16),
         vmem((head_count, cells, width), BF16),
         vmem((cells, group * C), F32),
@@ -563,7 +596,7 @@
     ]
     scratch += [dma((head_count, chips)) for _ in range(4)]
     scratch += [
-        dma((head_count, 2)), dma((head_count, 2)), dma((head_count,)), dma((head_count,)), dma((head_count, 2)),
+        dma((2, head_count, 2)), dma((2, head_count, 2)), dma((head_count,)), dma((head_count,)), dma((head_count, 2)),
         dma((head_count, 2)), dma((head_count, chips)), dma((head_count, chips)),
     ]
     return pl.pallas_call(

time: 84.2 us -> 78.5 us (0.932)
  Pallas kernels: 81 us -> 75.3 us
    pallas_call x1, Pallas kernels: 81 us -> 75.3 us  [body(): pl.pallas_call(functools.partial(kernel, region_count, head_count), out_s...]
where the time goes in v2:
time: 78.5 us; the launch traced here: 78.3 us
  Pallas kernels  75.3 us (96%)
  local copies, waits for them, and re-layouts  2.36 us (3%)
    pallas_call x1, Pallas kernels, body(): pl.pallas_call(functools.partial(kernel, region_count, head_count), out_s...  75.3 us
    unnamed x1, local copies, waits for them, and re-layouts  2.36 us

profile of v2, /device:TPU:0, one launch (start us, length us, event | category | flops | bytes accessed | tf_op | source)
XLA Modules:
  0.0 78.3 jit_solution(12447655912757229285)
XLA Ops:
  0.7 75.3 %shard_map.136 = f32[576,512]{1,0:T(8,128)} custom-call(s32[1]{0:T(128)S(6)} %copy.16.shift, s32[4]{0:T(128)} %counts.1, f32[576,512]{1,0:T(8,128)} %tokens.1, bf16[512,1536]{1,0:T(8,128)(2,1)} %w_qkv.1, bf16[512,512]{1,0:T(8,128)(2,1)} %w_proj.1, bf16[512,2048]{1,0:T(8,128)(2,1)} %w_up.1, bf16[2048,512]{1,0:T(8,128)(2,1)} %w_down.1, ...), custom_call_target="tpu_custom_call" | custom-call | tf_op jit(solution)/shard_map/pallas_call | solution.py:602
  76.0 2.4 %copy.17 = f32[576,512]{1,0:T(8,128)} copy(f32[576,512]{1,0:T(8,128)} %shard_map.136) | data formatting | bytes 2359296

commit v3 on v2

--- a/solution.py
+++ b/solution.py
@@ -67,15 +67,15 @@
 
 def kernel(
     region_count, head_count,
-    shift, counts, tokens, w_qkv, w_proj, w_up, w_down, w_merge,
+    shift, counts, tokens_in, w_qkv, w_proj, w_up, w_down, w_merge,
     c_qkv, c_proj, c_up, c_down, w_expand, w_out,
     out,
-    v_qkv, v_proj, v_up, v_down, v_merge, v_expand, v_out,
+    tokens, v_qkv, v_proj, v_up, v_down, v_merge, v_expand, v_out,
     g_qkv, g_proj, g_up, g_down,
     extended, rolled, packed, blended, fine, fine_bf, hidden,
     coarse, shared, sent_blend, got_blend, mid, c_normed, c_hidden, parts, got_parts,
     wide, spread, lanes,
-    local_sem, halo_send, halo_recv, own_sem, z_send, w_recv, p_send, q_send, q_recv, x_send, x_recv,
+    local_sem, halo_send, halo_recv, own_sem, z_send, z_recv, p_send, p_recv, q_send, q_recv, x_send, x_recv,
     a_send, a_recv, b_send, b_recv, m_send, m_recv, r_send, r_recv,
 ):
     region, head = lax.axis_index("region"), lax.axis_index("head")
@@ -115,6 +115,9 @@
             return g_up.at[pl.ds(owner * c_up.shape[0] + half_up, half_up)]
         return g_down.at[owner]
 
+    token_load = pltpu.make_async_copy(tokens_in, tokens, local_sem.at[7])
+    token_load.start()
+
     own_shards = []
     for which in range(5):
         own_shards.append(pltpu.make_async_copy(shards[which], slot(which, region), own_sem.at[which]))
@@ -133,13 +136,29 @@
             device_id=device, device_id_type=MESH,
         )
 
+    def received(place, sem):
+        remote(place, place, sem, sem, partner).wait_recv()
+
+    def sent(place, sem):
+        remote(place, place, sem, sem, partner).wait_send()
+
+    def stack(which, n):
+        if which == QKV:
+            return g_qkv.at[pl.ds(0, n * c_qkv.shape[0])]
+        if which == PROJ:
+            return g_proj.at[0, pl.ds(0, n)]
+        if which == DOWN:
+            return g_down.at[pl.ds(0, n)]
+        return g_up.at[pl.ds(0, n * half_up)]
+
+    token_load.wait()
     extended[WIN : WIN + rows, :] = norm(tokens[...]).astype(BF16)
     pl.semaphore_wait(barrier, len(greeted))
 
     halo_left = remote(extended.at[pl.ds(WIN, WIN)], extended.at[pl.ds(WIN + rows, WIN)],
-                       halo_send.at[0], halo_recv.at[0], before)
+                       halo_send, halo_recv, before)
     halo_right = remote(extended.at[pl.ds(rows, WIN)], extended.at[pl.ds(0, WIN)],
-                        halo_send.at[1], halo_recv.at[1], after)
+                        halo_send, halo_recv, after)
     halo_left.start()
     halo_right.start()
 
@@ -155,12 +174,12 @@
     def hop(which, way, far):
         owner = owner_of(way, far)
         place = slot(which, owner)
-        return remote(place, place,
-                      z_send.at[which, (way < 0) * chips + far], w_recv.at[which, owner], line(way))
+        return remote(place, place, z_send.at[which], z_recv.at[which, owner // 2], line(way))
 
     def pass_over(which, owner):
         place = slot(which, owner)
-        return remote(place, place, p_send.at[which, owner // 2], w_recv.at[which, owner], partner)
+        arrival = p_recv.at[which + owner // 2 if which == DOWN else which]
+        return remote(place, place, p_send.at[which], arrival, partner)
 
     def chip_at(s):
         if chips != 4:
@@ -172,7 +191,7 @@
         owner = chip_at(s) * 2 + core
         for k in range(1, head_count):
             piece = g_proj.at[head, owner]
-            remote(piece, piece, q_send.at[k, owner // 2], q_recv.at[k, owner // 2], plane[k]).start()
+            remote(piece, piece, q_send, q_recv, plane[k]).start()
 
     def send_own(which):
         for way in ways:
@@ -182,8 +201,7 @@
 
     def arrive(which, way, far, forward):
         owner = owner_of(way, far)
-        remote(slot(which, owner), slot(which, owner), p_send.at[which, owner // 2],
-               w_recv.at[which, owner], line(way)).wait_recv()
+        received(slot(which, owner), z_recv.at[which, owner // 2])
         if forward:
             hop(which, way, far).start()
         pass_over(which, owner).start()
@@ -203,13 +221,8 @@
                 def _():
                     arrive(which, way, far, False)
 
-    def take_one(which, owner):
-        remote(slot(which, owner), slot(which, owner), p_send.at[which, owner // 2],
-               w_recv.at[which, owner], partner).wait_recv()
-
     def take_over(which):
-        for s in range(chips):
-            take_one(which, ((chip + s) % chips) * 2 + 1 - core)
+        received(stack(which, chips), p_recv.at[which])
 
     fars = range(1, chips)
 
@@ -227,38 +240,27 @@
         half = whole.shape[1] // 2
         return whole.at[:, pl.ds(i * half, half)]
 
-    def half_copy(piece_of, h, k, i, send, recv):
-        piece = half_of(piece_of, h, i)
-        return remote(piece, piece, send.at[k, i], recv.at[k, i], plane[k])
-
     def gather(piece_of, send, recv):
-        copies = []
         for i in range(2):
             for k in range(1, 3 if relay else head_count):
-                copy = half_copy(piece_of, head, k, i if k != 2 else 1 - i, send, recv)
-                copy.start()
-                copies.append(copy)
-        return copies
-
-    def far_half(piece_of, mask, i, send, recv, device):
-        piece = half_of(piece_of, flip(head, mask), i)
-        return remote(piece, piece, send.at[3, i], recv.at[3, i], device)
-
-    def hand_on(piece_of, send, recv, copies):
+                which = i if k != 2 else 1 - i
+                piece = half_of(piece_of, head, which)
+                lane = recv.at[(k - 1 if which == k - 1 else 2) if relay else k]
+                remote(piece, piece, send, lane, plane[k]).start()
+
+    def hand_on(piece_of, send, recv):
         if not relay:
             return
         for i, (came_by, goes_by) in enumerate(((1, 2), (2, 1))):
-            half_copy(piece_of, flip(head, came_by), came_by, i, send, recv).wait_recv()
-            copy = far_half(piece_of, came_by, i, send, recv, plane[goes_by])
-            copy.start()
-            copies.append(copy)
-
-    def arrived(piece_of, k, send, recv):
-        for i in range(2):
-            if relay and k == 3:
-                far_half(piece_of, 3, i, send, recv, plane[2 - i]).wait_recv()
-            elif not (relay and i == k - 1):
-                half_copy(piece_of, flip(head, k), k, i, send, recv).wait_recv()
+            piece = half_of(piece_of, flip(head, came_by), i)
+            received(piece, recv.at[i])
+            remote(piece, piece, send, recv.at[3], plane[goes_by]).start()
+
+    def arrived(piece_of, k, recv):
+        if not relay or k == 3:
+            received(piece_of(flip(head, k)), recv.at[k])
+        elif k == 1:
+            received(piece_of(head), recv.at[2])
 
     offset = shift[0]
     at_row = lax.broadcasted_iota(jnp.int32, (WIN, 2 * WIN), 0)
@@ -339,9 +341,8 @@
     fine_chunk(0)
     forward(QKV, 1)
     merge_chunk(0)
-    gathers = gather(shared_of(0), a_send.at[0], a_recv.at[0])
-    halo_left.wait()
-    halo_right.wait()
+    gather(shared_of(0), a_send, a_recv.at[0])
+    received(extended.at[pl.ds(0, 2 * WIN)], halo_recv)
     forward(PROJ, 1)
     collect(PROJ, fars[:1])
     for s in range(min(2, chips)):
@@ -356,12 +357,12 @@
         own_shards[which].wait()
         pass_over(which, region).start()
     send_own(UP0)
-    hand_on(shared_of(0), a_send.at[0], a_recv.at[0], gathers)
+    hand_on(shared_of(0), a_send, a_recv.at[0])
     fine_chunk(1)
     for far in fars[1:]:
         forward(PROJ, far)
     merge_chunk(1)
-    gathers += gather(shared_of(1), a_send.at[1], a_recv.at[1])
+    gather(shared_of(1), a_send, a_recv.at[1])
     send_own(UP1)
     collect(QKV, fars)
     take_over(QKV)
@@ -373,7 +374,6 @@
         at_key < inside, at_key + block_cells, jnp.where(at_key < inside + block_cells, at_key - inside, at_key)
     )
 
-    blends = []
     heads_here = g_qkv.shape[1] // (3 * HD)
 
     def coarse_attention(ks):
@@ -392,7 +392,7 @@
 
     forward(UP0, 1)
     coarse_attention([0])
-    hand_on(shared_of(1), a_send.at[1], a_recv.at[1], gathers)
+    hand_on(shared_of(1), a_send, a_recv.at[1])
     collect(PROJ, fars[1:])
     for s in range(2, chips):
         spread_proj(s)
@@ -403,30 +403,24 @@
     for ks in [range(1, min(3, head_count)), range(3, head_count)]:
         for k in ks:
             for index in range(2):
-                arrived(shared_of(index), k, a_send.at[index], a_recv.at[index])
+                arrived(shared_of(index), k, a_recv.at[index])
         coarse_attention(ks)
         for k in ks:
-            copy = remote(sent_blend.at[k], got_blend.at[head], b_send.at[k], b_recv.at[k], plane[k])
-            copy.start()
-            blends.append(copy)
+            remote(sent_blend.at[k], got_blend.at[head], b_send, b_recv, plane[k]).start()
         if 1 in ks:
             for far in fars[1:]:
                 forward(UP1, far)
     forward(DOWN, 1)
+    others = pl.ds(0, head_count - 1)
+    received(g_proj.at[others, pl.ds(0, chips)], q_recv)
     for s in range(chips):
-        owner = ((chip + s) % chips) * 2 + core
+        owner = chip_at(s) * 2 + core
         for k in range(1, head_count):
             piece = g_proj.at[plane[k][1], owner]
-            remote(piece, piece, q_send.at[k, s], q_recv.at[k, owner // 2], plane[k]).wait_recv()
-            remote(piece, piece, x_send.at[k, s], x_recv.at[k, owner // 2], partner).start()
+            remote(piece, piece, x_send, x_recv, partner).start()
     take_over(PROJ)
-    for s in range(chips):
-        owner = ((chip + s) % chips) * 2 + 1 - core
-        for k in range(1, head_count):
-            piece = g_proj.at[plane[k][1], owner]
-            remote(piece, piece, x_send.at[k, s], x_recv.at[k, owner // 2], partner).wait_recv()
-    for copy in blends:
-        copy.wait_recv()
+    received(g_proj.at[others, pl.ds(0, chips)], x_recv)
+    received(got_blend.at[others], b_recv)
     for r in range(region_count):
         w = g_proj.shape[3]
         total_of = dot(got_blend[0], g_proj[0, r])
@@ -441,7 +435,7 @@
         return c_normed.at[row_block(h)]
 
     c_normed[row_block(head), :] = norm(mid[...]).astype(BF16)
-    seconds = gather(normed_of, m_send, m_recv)
+    gather(normed_of, m_send, m_recv)
     for far in fars[1:]:
         forward(DOWN, far)
     own[5].wait()
@@ -449,13 +443,12 @@
     for c in range(C // 256):
         at = slice(c * 256, (c + 1) * 256)
         fine[:, at] = dot(fine_bf[...], v_out[:C, at])
-    hand_on(normed_of, m_send, m_recv, seconds)
+    hand_on(normed_of, m_send, m_recv)
     for which in (UP0, UP1):
         collect(which, fars)
         take_over(which)
     w = g_down.shape[2]
     pair = 2 * w
-    returns = []
 
     def columns_of(s):
         return pl.ds(pl.multiple_of(chip_at(s) * pair, pair), pair)
@@ -468,7 +461,7 @@
                     @pl.when(came(way, far) & jnp.logical_not(goes(way)) & (owner_of(way, far) // 2 == holder))
                     def _():
                         arrive(DOWN, way, far, False)
-        take_one(DOWN, holder * 2 + 1 - core)
+        received(slot(DOWN, holder * 2 + 1 - core), p_recv.at[DOWN + holder])
 
     def down(k, s):
         holder = chip_at(s)
@@ -480,16 +473,14 @@
             parts[k, :, columns_of(s)] = product.astype(BF16)
 
     def send_back(k, s):
-        copy = remote(parts.at[k, :, columns_of(s)], got_parts.at[k, :, columns_of(s)],
-                      r_send.at[k, s], r_recv.at[k, s], plane[k])
-        copy.start()
-        returns.append(copy)
+        remote(parts.at[k, :, columns_of(s)], got_parts.at[k - 1, :, columns_of(s)],
+               r_send, r_recv.at[s], plane[k]).start()
 
     early = min(2, chips)
     for k in range(head_count):
         at = row_block(plane[k][1])
         if k > 0:
-            arrived(normed_of, k, m_send, m_recv)
+            arrived(normed_of, k, m_recv)
         c_hidden[at, :] = gelu(dot(c_normed[at, :], g_up[...])).astype(BF16)
         for s in range(early):
             if k == 0:
@@ -506,12 +497,10 @@
                 send_back(k, s)
     for s in range(chips):
         columns = columns_of(s)
-        for k in range(1, head_count):
-            remote(parts.at[k, :, columns], got_parts.at[k, :, columns],
-                   r_send.at[k, s], r_recv.at[k, s], plane[k]).wait_recv()
+        received(got_parts.at[others, :, columns], r_recv.at[s])
         result = mid[:, columns]
         for k in range(1, head_count):
-            result += got_parts[k, :, columns].astype(F32)
+            result += got_parts[k - 1, :, columns].astype(F32)
         result = result.astype(BF16)
         for k in range(group):
             at = slice(k * C, (k + 1) * C)
@@ -534,26 +523,22 @@
         for p, j in enumerate(order):
             out[j * WIN : (j + 1) * WIN, at] = lanes[c, p * WIN : (p + 1) * WIN, :]
 
-    for copy in gathers + blends + seconds + returns:
-        copy.wait_send()
+    sent(extended.at[pl.ds(0, 2 * WIN)], halo_send)
+    sent(shared.at[pl.ds(0, 2), others], a_send)
+    sent(g_proj.at[others, pl.ds(0, chips)], q_send)
+    sent(g_proj.at[others, pl.ds(0, chips)], x_send)
+    sent(sent_blend.at[others], b_send)
+    sent(c_normed.at[pl.ds(0, (head_count - 1) * cells)], m_send)
+    sent(parts.at[others], r_send)
     for which in range(5):
-        for way in ways:
-            @pl.when(goes(way))
-            def _():
-                hop(which, way, 0).wait_send()
-            for far in fars[:-1]:
-                @pl.when(came(way, far) & goes(way))
-                def _():
-                    hop(which, way, far).wait_send()
-        for s in range(chips):
-            pass_over(which, ((chip + s) % chips) * 2 + core).wait_send()
-    for s in range(chips):
-        owner = ((chip + s) % chips) * 2 + core
-        for k in range(1, head_count):
-            piece = g_proj.at[head, owner]
-            remote(piece, piece, q_send.at[k, owner // 2], q_recv.at[k, owner // 2], plane[k]).wait_send()
-            piece = g_proj.at[plane[k][1], owner]
-            remote(piece, piece, x_send.at[k, s], x_recv.at[k, owner // 2], partner).wait_send()
+        sent(stack(which, chips), p_send.at[which])
+    for place in range(chips):
+        hops = (place + 1) * (place < chips - 1) + (chips - place) * (place > 0)
+
+        @pl.when(chip == place)
+        def _():
+            for which in range(5):
+                sent(stack(which, hops), z_send.at[which])
 
 
 def body(region_count, head_count, tokens, shift, counts, *weights):
@@ -563,11 +548,11 @@
     group = w_merge.shape[0] // C
     cells = rows // group
     vmem = pltpu.VMEM
-    any_spec = pl.BlockSpec(memory_space=pl.ANY)
     dma = pltpu.SemaphoreType.DMA
     chips = region_count // 2
     mine = c_proj.shape[0]
-    scratch = [vmem(w.shape, BF16) for w in (w_qkv, w_proj, w_up, w_down, w_merge, w_expand, w_out)]
+    scratch = [vmem(tokens.shape, F32)]
+    scratch += [vmem(w.shape, BF16) for w in (w_qkv, w_proj, w_up, w_down, w_merge, w_expand, w_out)]
     scratch += [
         vmem((width, c_qkv.shape[1]), BF16),
         vmem((head_count, region_count) + c_proj.shape, BF16),
@@ -592,24 +577,21 @@
         vmem((cells, group * C), F32),
         vmem((rows, C), BF16),
         vmem((C // 128, rows, 128), F32),
-        dma((7,)), dma((2,)), dma((2,)), dma((5,)), dma((5, 2 * chips)), dma((5, region_count)), dma((5, chips)),
+        dma((8,)), dma, dma, dma((5,)), dma((5,)), dma((5, chips)), dma((5,)), dma((4 + chips,)), dma, dma, dma, dma,
+        dma, dma((2, max(head_count, 4))), dma, dma, dma, dma((max(head_count, 4),)), dma, dma((chips,)),
     ]
-    scratch += [dma((head_count, chips)) for _ in range(4)]
-    scratch += [
-        dma((2, head_count, 2)), dma((2, head_count, 2)), dma((head_count,)), dma((head_count,)), dma((head_count, 2)),
-        dma((head_count, 2)), dma((head_count, chips)), dma((head_count, chips)),
-    ]
+    placed = [pltpu.with_memory_space_constraint(w, pltpu.HBM) for w in (tokens,) + weights]
     return pl.pallas_call(
         functools.partial(kernel, region_count, head_count),
         out_shape=jax.ShapeDtypeStruct((rows, C), F32),
         in_specs=[pl.BlockSpec(memory_space=pltpu.SMEM)] * 2
-        + [pl.BlockSpec(memory_space=pltpu.VMEM)] + [any_spec] * 11,
+        + [pl.BlockSpec(memory_space=pltpu.HBM)] * len(placed),
         out_specs=pl.BlockSpec(memory_space=pltpu.VMEM),
         scratch_shapes=scratch,
         compiler_params=pltpu.CompilerParams(
-            collective_id=0, has_side_effects=True, vmem_limit_bytes=60 * 1024 * 1024
+            collective_id=0, has_side_effects=True, vmem_limit_bytes=50 * 1024 * 1024
         ),
-    )(shift, counts, tokens, *weights)
+    )(shift, pltpu.with_memory_space_constraint(counts, pltpu.HBM), *placed)
 
 
 def solution(mesh):

time: 78.5 us -> 73.4 us (0.935)
  Pallas kernels: 75.3 us -> 71.4 us
  local copies, waits for them, and re-layouts: 2.36 us -> 1.02 us
    pallas_call x1, Pallas kernels: 75.3 us -> 71.4 us  [body(): pl.pallas_call(functools.partial(kernel, region_count, head_count), out_s...]
    unnamed x1, local copies, waits for them, and re-layouts: 2.36 us -> 1.02 us
where the time goes in v3:
time: 73.4 us; the launch traced here: 73 us
  Pallas kernels  71.4 us (97%)
  local copies, waits for them, and re-layouts  1.02 us (1%)
    pallas_call x1, Pallas kernels, body(): pl.pallas_call(functools.partial(kernel, region_count, head_count), out_s...  71.4 us

profile of v3, /device:TPU:0, one launch (start us, length us, event | category | flops | bytes accessed | tf_op | source)
XLA Modules:
  0.0 73.0 jit_solution(2909623463576165390)
XLA Ops:
  0.7 71.4 %shard_map.136 = f32[576,512]{1,0:T(8,128)S(1)} custom-call(s32[1]{0:T(128)S(6)} %copy.16.shift, s32[4]{0:T(128)} %counts.1, f32[576,512]{1,0:T(8,128)} %tokens_in.1, bf16[512,1536]{1,0:T(8,128)(2,1)} %w_qkv.1, bf16[512,512]{1,0:T(8,128)(2,1)} %w_proj.1, bf16[512,2048]{1,0:T(8,128)(2,1)} %w_up.1, bf16[2048,512]{1,0:T(8,128)(2,1)} %w_down.1, ...), custom_call_target="tpu_custom_call" | custom-call | tf_op jit(solution)/shard_map/pallas_call | solution.py:584
  72.0 1.0 %copy.17 = f32[576,512]{1,0:T(8,128)} copy(f32[576,512]{1,0:T(8,128)S(1)} %shard_map.136) | data formatting | bytes 2359296

commit v4 on v3

--- a/solution.py
+++ b/solution.py
@@ -100,13 +100,14 @@
     for device in greeted:
         pl.semaphore_signal(barrier, inc=1, device_id=device, device_id_type=MESH)
 
-    QKV, PROJ, UP0, UP1, DOWN = range(5)
-    half_up = c_up.shape[0] // 2
-    shards = [c_qkv, c_proj, c_up.at[pl.ds(0, half_up)], c_up.at[pl.ds(half_up, half_up)], c_down]
+    PROJ, QKV0, QKV1, UP0, UP1, DOWN = range(6)
+    half_qkv, half_up = c_qkv.shape[0] // 2, c_up.shape[0] // 2
+    shards = [c_proj, c_qkv.at[pl.ds(0, half_qkv)], c_qkv.at[pl.ds(half_qkv, half_qkv)],
+              c_up.at[pl.ds(0, half_up)], c_up.at[pl.ds(half_up, half_up)], c_down]
 
     def slot(which, owner):
-        if which == QKV:
-            return g_qkv.at[pl.ds(owner * c_qkv.shape[0], c_qkv.shape[0])]
+        if which in (QKV0, QKV1):
+            return g_qkv.at[pl.ds(owner * c_qkv.shape[0] + (which - QKV0) * half_qkv, half_qkv)]
         if which == PROJ:
             return g_proj.at[head, owner]
         if which == UP0:
@@ -119,7 +120,7 @@
     token_load.start()
 
     own_shards = []
-    for which in range(5):
+    for which in range(6):
         own_shards.append(pltpu.make_async_copy(shards[which], slot(which, region), own_sem.at[which]))
     own = []
     for at, (source, target) in enumerate(
@@ -127,7 +128,7 @@
          (w_expand, v_expand), (w_out, v_out)]
     ):
         own.append(pltpu.make_async_copy(source, target, local_sem.at[at]))
-    for copy in (own_shards[0], own_shards[1], own[0], own[1]):
+    for copy in (*own_shards[:3], own[0], own[1]):
         copy.start()
 
     def remote(source, target, send, recv, device):
@@ -143,8 +144,8 @@
         remote(place, place, sem, sem, partner).wait_send()
 
     def stack(which, n):
-        if which == QKV:
-            return g_qkv.at[pl.ds(0, n * c_qkv.shape[0])]
+        if which in (QKV0, QKV1):
+            return g_qkv.at[pl.ds(0, n * half_qkv)]
         if which == PROJ:
             return g_proj.at[0, pl.ds(0, n)]
         if which == DOWN:
@@ -191,7 +192,7 @@
         owner = chip_at(s) * 2 + core
         for k in range(1, head_count):
             piece = g_proj.at[head, owner]
-            remote(piece, piece, q_send, q_recv, plane[k]).start()
+            remote(piece, piece, q_send, q_recv.at[s // 2], plane[k]).start()
 
     def send_own(which):
         for way in ways:
@@ -225,12 +226,21 @@
         received(stack(which, chips), p_recv.at[which])
 
     fars = range(1, chips)
-
-    for which in (QKV, PROJ):
+    others = pl.ds(0, head_count - 1)
+
+    def pass_proj(part):
+        these = range(2 * part, min(2 * part + 2, chips))
+        received(g_proj.at[others, pl.ds(0, len(these))], q_recv.at[part])
+        for s in these:
+            for k in range(1, head_count):
+                piece = g_proj.at[plane[k][1], chip_at(s) * 2 + core]
+                remote(piece, piece, x_send, x_recv, partner).start()
+
+    for which in (PROJ, QKV0, QKV1):
         own_shards[which].wait()
         send_own(which)
         pass_over(which, region).start()
-    for copy in own[2:5] + own_shards[2:] + own[5:]:
+    for copy in own[2:5] + own_shards[3:] + own[5:]:
         copy.start()
 
     relay = head_count == 4
@@ -339,33 +349,47 @@
     project_rows(0, inner * WIN)
     windows(0, inner)
     fine_chunk(0)
-    forward(QKV, 1)
+    spread_proj(0)
+    forward(PROJ, 1)
+    forward(QKV0, 1)
     merge_chunk(0)
     gather(shared_of(0), a_send, a_recv.at[0])
+    forward(QKV1, 1)
     received(extended.at[pl.ds(0, 2 * WIN)], halo_recv)
-    forward(PROJ, 1)
     collect(PROJ, fars[:1])
-    for s in range(min(2, chips)):
-        spread_proj(s)
+    for far in fars[1:]:
+        forward(PROJ, far)
+    for which in (UP0, UP1, DOWN):
+        own_shards[which].wait()
+        pass_over(which, region).start()
+    send_own(UP0)
     roll_window(0)
     roll_window(blocks)
     project_rows(inner * WIN, (blocks + 1) * WIN)
     windows(inner, blocks + 1)
+    hand_on(shared_of(0), a_send, a_recv.at[0])
+    for s in range(1, min(2, chips)):
+        spread_proj(s)
     for far in fars[1:]:
-        forward(QKV, far)
-    for which in (UP0, UP1, DOWN):
-        own_shards[which].wait()
-        pass_over(which, region).start()
-    send_own(UP0)
-    hand_on(shared_of(0), a_send, a_recv.at[0])
+        forward(QKV0, far)
     fine_chunk(1)
     for far in fars[1:]:
-        forward(PROJ, far)
+        forward(QKV1, far)
+    send_own(UP1)
     merge_chunk(1)
     gather(shared_of(1), a_send, a_recv.at[1])
-    send_own(UP1)
-    collect(QKV, fars)
-    take_over(QKV)
+    forward(UP0, 1)
+    hand_on(shared_of(1), a_send, a_recv.at[1])
+    collect(PROJ, fars[1:])
+    for s in range(2, chips):
+        spread_proj(s)
+    forward(UP1, 1)
+    for which in (QKV0, QKV1):
+        collect(which, fars[:2])
+    for which in (QKV0, QKV1):
+        collect(which, fars[2:])
+    for which in (QKV0, QKV1):
+        take_over(which)
 
     at_key = lax.broadcasted_iota(jnp.int32, (cells, cells), 0)
     block_cells = WIN // group
@@ -390,16 +414,10 @@
             else:
                 sent_blend[k] = jnp.concatenate(parts_of, axis=1)
 
-    forward(UP0, 1)
+    pass_proj(0)
     coarse_attention([0])
-    hand_on(shared_of(1), a_send, a_recv.at[1])
-    collect(PROJ, fars[1:])
-    for s in range(2, chips):
-        spread_proj(s)
-    forward(UP1, 1)
     for far in fars[1:]:
         forward(UP0, far)
-    send_own(DOWN)
     for ks in [range(1, min(3, head_count)), range(3, head_count)]:
         for k in ks:
             for index in range(2):
@@ -408,16 +426,11 @@
         for k in ks:
             remote(sent_blend.at[k], got_blend.at[head], b_send, b_recv, plane[k]).start()
         if 1 in ks:
-            for far in fars[1:]:
-                forward(UP1, far)
-    forward(DOWN, 1)
-    others = pl.ds(0, head_count - 1)
-    received(g_proj.at[others, pl.ds(0, chips)], q_recv)
-    for s in range(chips):
-        owner = chip_at(s) * 2 + core
-        for k in range(1, head_count):
-            piece = g_proj.at[plane[k][1], owner]
-            remote(piece, piece, x_send, x_recv, partner).start()
+            send_own(DOWN)
+    for far in fars[1:]:
+        forward(UP1, far)
+    for part in range(1, (chips + 1) // 2):
+        pass_proj(part)
     take_over(PROJ)
     received(g_proj.at[others, pl.ds(0, chips)], x_recv)
     received(got_blend.at[others], b_recv)
@@ -436,31 +449,30 @@
 
     c_normed[row_block(head), :] = norm(mid[...]).astype(BF16)
     gather(normed_of, m_send, m_recv)
-    for far in fars[1:]:
-        forward(DOWN, far)
+    collect(UP0, fars)
+    collect(UP1, fars[:1])
+    forward(DOWN, 1)
     own[5].wait()
     own[6].wait()
     for c in range(C // 256):
         at = slice(c * 256, (c + 1) * 256)
         fine[:, at] = dot(fine_bf[...], v_out[:C, at])
     hand_on(normed_of, m_send, m_recv)
-    for which in (UP0, UP1):
-        collect(which, fars)
-        take_over(which)
     w = g_down.shape[2]
     pair = 2 * w
 
     def columns_of(s):
         return pl.ds(pl.multiple_of(chip_at(s) * pair, pair), pair)
 
-    def down_ready(s):
+    def down_collect(s):
+        for far in fars:
+            for way in ways:
+                @pl.when(came(way, far) & jnp.logical_not(goes(way)) & (owner_of(way, far) // 2 == chip_at(s)))
+                def _():
+                    arrive(DOWN, way, far, False)
+
+    def down_take(s):
         holder = chip_at(s)
-        if s > 0:
-            for far in fars:
-                for way in ways:
-                    @pl.when(came(way, far) & jnp.logical_not(goes(way)) & (owner_of(way, far) // 2 == holder))
-                    def _():
-                        arrive(DOWN, way, far, False)
         received(slot(DOWN, holder * 2 + 1 - core), p_recv.at[DOWN + holder])
 
     def down(k, s):
@@ -477,20 +489,33 @@
                r_send, r_recv.at[s], plane[k]).start()
 
     early = min(2, chips)
+    collect(UP1, fars[1:])
+    for s in range(1, early):
+        down_collect(s)
+    for which in (UP0, UP1):
+        take_over(which)
     for k in range(head_count):
         at = row_block(plane[k][1])
         if k > 0:
             arrived(normed_of, k, m_recv)
+        if k == 1:
+            for far in fars[1:]:
+                forward(DOWN, far)
         c_hidden[at, :] = gelu(dot(c_normed[at, :], g_up[...])).astype(BF16)
+        if k == 2:
+            for s in range(early, min(early + 1, chips)):
+                down_collect(s)
         for s in range(early):
             if k == 0:
-                down_ready(s)
+                down_take(s)
         for s in range(early):
             down(k, s)
             if k > 0:
                 send_back(k, s)
     for s in range(early, chips):
-        down_ready(s)
+        if s > early or head_count < 3:
+            down_collect(s)
+        down_take(s)
         for k in [*range(1, head_count), 0]:
             down(k, s)
             if k > 0:
@@ -530,14 +555,14 @@
     sent(sent_blend.at[others], b_send)
     sent(c_normed.at[pl.ds(0, (head_count - 1) * cells)], m_send)
     sent(parts.at[others], r_send)
-    for which in range(5):
+    for which in range(6):
         sent(stack(which, chips), p_send.at[which])
     for place in range(chips):
         hops = (place + 1) * (place < chips - 1) + (chips - place) * (place > 0)
 
         @pl.when(chip == place)
         def _():
-            for which in range(5):
+            for which in range(6):
                 sent(stack(which, hops), z_send.at[which])
 
 
@@ -577,7 +602,7 @@
         vmem((cells, group * C), F32),
         vmem((rows, C), BF16),
         vmem((C // 128, rows, 128), F32),
-        dma((8,)), dma, dma, dma((5,)), dma((5,)), dma((5, chips)), dma((5,)), dma((4 + chips,)), dma, dma, dma, dma,
+        dma((8,)), dma, dma, dma((6,)), dma((6,)), dma((6, chips)), dma((6,)), dma((5 + chips,)), dma, dma(((chips + 1) // 2,)), dma, dma,
         dma, dma((2, max(head_count, 4))), dma, dma, dma, dma((max(head_count, 4),)), dma, dma((chips,)),
     ]
     placed = [pltpu.with_memory_space_constraint(w, pltpu.HBM) for w in (tokens,) + weights]

time: 73.4 us -> 70.4 us (0.959)
  Pallas kernels: 71.4 us -> 68.6 us
    pallas_call x1, Pallas kernels: 71.4 us -> 68.6 us  [body(): pl.pallas_call(functools.partial(kernel, region_count, head_count), out_s...]
where the time goes in v4:
time: 70.4 us; the launch traced here: 70.3 us
  Pallas kernels  68.6 us (97%)
  local copies, waits for them, and re-layouts  1.02 us (1%)
    pallas_call x1, Pallas kernels, body(): pl.pallas_call(functools.partial(kernel, region_count, head_count), out_s...  68.6 us

profile of v4, /device:TPU:0, one launch (start us, length us, event | category | flops | bytes accessed | tf_op | source)
XLA Modules:
  0.0 70.3 jit_solution(9301383966958521724)
XLA Ops:
  0.7 68.6 %shard_map.136 = f32[576,512]{1,0:T(8,128)S(1)} custom-call(s32[1]{0:T(128)S(6)} %copy.16.shift, s32[4]{0:T(128)} %counts.1, f32[576,512]{1,0:T(8,128)} %tokens_in.1, bf16[512,1536]{1,0:T(8,128)(2,1)} %w_qkv.1, bf16[512,512]{1,0:T(8,128)(2,1)} %w_proj.1, bf16[512,2048]{1,0:T(8,128)(2,1)} %w_up.1, bf16[2048,512]{1,0:T(8,128)(2,1)} %w_down.1, ...), custom_call_target="tpu_custom_call" | custom-call | tf_op jit(solution)/shard_map/pallas_call | solution.py:609
  69.3 1.0 %copy.17 = f32[576,512]{1,0:T(8,128)} copy(f32[576,512]{1,0:T(8,128)S(1)} %shard_map.136) | data formatting | bytes 2359296

commit v5 on v4

--- a/solution.py
+++ b/solution.py
@@ -73,7 +73,7 @@
     tokens, v_qkv, v_proj, v_up, v_down, v_merge, v_expand, v_out,
     g_qkv, g_proj, g_up, g_down,
     extended, rolled, packed, blended, fine, fine_bf, hidden,
-    coarse, shared, sent_blend, got_blend, mid, c_normed, c_hidden, parts, got_parts,
+    coarse, shared, c_packed, sent_blend, got_blend, mid, c_normed, c_hidden, parts, got_parts,
     wide, spread, lanes,
     local_sem, halo_send, halo_recv, own_sem, z_send, z_recv, p_send, p_recv, q_send, q_recv, x_send, x_recv,
     a_send, a_recv, b_send, b_recv, m_send, m_recv, r_send, r_recv,
@@ -400,39 +400,30 @@
 
     heads_here = g_qkv.shape[1] // (3 * HD)
 
-    def coarse_attention(ks):
-        packed_of = [
-            jnp.concatenate(
-                [dot(shared[index, plane[k][1]], g_qkv[...]) for index in range(2)], axis=0
-            ).astype(BF16)
-            for k in ks
-        ]
-        for k, its in zip(ks, packed_of):
-            parts_of = attend(its, heads_here, place < counts[plane[k][1]])
-            if k == 0:
-                got_blend[head] = jnp.concatenate(parts_of, axis=1)
-            else:
-                sent_blend[k] = jnp.concatenate(parts_of, axis=1)
-
     pass_proj(0)
-    coarse_attention([0])
     for far in fars[1:]:
         forward(UP0, far)
-    for ks in [range(1, min(3, head_count)), range(3, head_count)]:
-        for k in ks:
-            for index in range(2):
-                arrived(shared_of(index), k, a_recv.at[index])
-        coarse_attention(ks)
-        for k in ks:
-            remote(sent_blend.at[k], got_blend.at[head], b_send, b_recv, plane[k]).start()
-        if 1 in ks:
-            send_own(DOWN)
+    for k in range(1, head_count):
+        for index in range(2):
+            arrived(shared_of(index), k, a_recv.at[index])
+    gathered = jnp.concatenate(
+        [shared[index, plane[k][1]] for k in range(head_count) for index in range(2)], axis=0
+    )
+    c_packed[...] = dot(gathered, g_qkv[...]).astype(BF16)
+    for k in range(head_count):
+        parts_of = attend(c_packed[k * cells : (k + 1) * cells, :], heads_here, place < counts[plane[k][1]])
+        sent_blend[k] = jnp.concatenate(parts_of, axis=1)
+    for k in range(head_count - 1, 0, -1):
+        remote(sent_blend.at[k], got_blend.at[head], b_send, b_recv, plane[k]).start()
+    got_blend[head] = sent_blend[0]
+    send_own(DOWN)
     for far in fars[1:]:
         forward(UP1, far)
     for part in range(1, (chips + 1) // 2):
         pass_proj(part)
     take_over(PROJ)
     received(g_proj.at[others, pl.ds(0, chips)], x_recv)
+    forward(DOWN, 1)
     received(got_blend.at[others], b_recv)
     for r in range(region_count):
         w = g_proj.shape[3]
@@ -451,25 +442,27 @@
     gather(normed_of, m_send, m_recv)
     collect(UP0, fars)
     collect(UP1, fars[:1])
-    forward(DOWN, 1)
     own[5].wait()
     own[6].wait()
     for c in range(C // 256):
         at = slice(c * 256, (c + 1) * 256)
         fine[:, at] = dot(fine_bf[...], v_out[:C, at])
-    hand_on(normed_of, m_send, m_recv)
-    w = g_down.shape[2]
-    pair = 2 * w
-
-    def columns_of(s):
-        return pl.ds(pl.multiple_of(chip_at(s) * pair, pair), pair)
-
     def down_collect(s):
         for far in fars:
             for way in ways:
                 @pl.when(came(way, far) & jnp.logical_not(goes(way)) & (owner_of(way, far) // 2 == chip_at(s)))
                 def _():
                     arrive(DOWN, way, far, False)
+
+    collect(UP1, fars[1:])
+    for s in range(1, min(2, chips)):
+        down_collect(s)
+    hand_on(normed_of, m_send, m_recv)
+    w = g_down.shape[2]
+    pair = 2 * w
+
+    def columns_of(s):
+        return pl.ds(pl.multiple_of(chip_at(s) * pair, pair), pair)
 
     def down_take(s):
         holder = chip_at(s)
@@ -489,18 +482,14 @@
                r_send, r_recv.at[s], plane[k]).start()
 
     early = min(2, chips)
-    collect(UP1, fars[1:])
-    for s in range(1, early):
-        down_collect(s)
     for which in (UP0, UP1):
         take_over(which)
+    for far in fars[1:]:
+        forward(DOWN, far)
     for k in range(head_count):
         at = row_block(plane[k][1])
         if k > 0:
             arrived(normed_of, k, m_recv)
-        if k == 1:
-            for far in fars[1:]:
-                forward(DOWN, far)
         c_hidden[at, :] = gelu(dot(c_normed[at, :], g_up[...])).astype(BF16)
         if k == 2:
             for s in range(early, min(early + 1, chips)):
@@ -516,7 +505,7 @@
         if s > early or head_count < 3:
             down_collect(s)
         down_take(s)
-        for k in [*range(1, head_count), 0]:
+        for k in [*range(head_count - 1, 0, -1), 0]:
             down(k, s)
             if k > 0:
                 send_back(k, s)
@@ -538,15 +527,18 @@
         spread[first:last, :] = jnp.concatenate(
             [wide[low:high, k * C : (k + 1) * C] for k in range(group)], axis=0
         ).astype(BF16)
-    for c in range(C // 128):
-        at = slice(c * 128, (c + 1) * 128)
-        value = fine[:, at] + dot(spread[...], v_out[C:, at])
-        for first, last in spans:
-            count = (last - first) // group
-            for k in range(group):
-                lanes[c, pl.ds(first + k, count, stride=group), :] = value[first + k * count : first + (k + 1) * count, :]
-        for p, j in enumerate(order):
-            out[j * WIN : (j + 1) * WIN, at] = lanes[c, p * WIN : (p + 1) * WIN, :]
+    for c in range(C // 256):
+        value = fine[:, c * 256 : (c + 1) * 256] + dot(spread[...], v_out[C:, c * 256 : (c + 1) * 256])
+        for lane in (2 * c, 2 * c + 1):
+            half = slice((lane - 2 * c) * 128, (lane - 2 * c + 1) * 128)
+            for first, last in spans:
+                count = (last - first) // group
+                for k in range(group):
+                    lanes[lane, pl.ds(first + k, count, stride=group), :] = value[
+                        first + k * count : first + (k + 1) * count, half
+                    ]
+            for p, j in enumerate(order):
+                out[j * WIN : (j + 1) * WIN, lane * 128 : (lane + 1) * 128] = lanes[lane, p * WIN : (p + 1) * WIN, :]
 
     sent(extended.at[pl.ds(0, 2 * WIN)], halo_send)
     sent(shared.at[pl.ds(0, 2), others], a_send)
@@ -592,6 +584,7 @@
         vmem((rows, w_up.shape[1]), BF16),
         vmem((cells, width), F32),
         vmem((2, head_count, cells // 2, width), BF16),
+        vmem((head_count * cells, c_qkv.shape[1]), BF16),
         vmem((head_count, cells, mine), BF16),
         vmem((head_count, cells, mine), BF16),
         vmem((cells, width), F32),

time: 70.4 us -> 70.2 us (level)
  no operation moved by 1% of the time
where the time goes in v5:
time: 70.2 us; the launch traced here: 70 us
  Pallas kernels  68.3 us (97%)
  local copies, waits for them, and re-layouts  1.02 us (1%)
    pallas_call x1, Pallas kernels, body(): pl.pallas_call(functools.partial(kernel, region_count, head_count), out_s...  68.3 us

profile of v5, /device:TPU:0, one launch (start us, length us, event | category | flops | bytes accessed | tf_op | source)
XLA Modules:
  0.0 70.0 jit_solution(4253350074299363768)
XLA Ops:
  0.7 68.3 %shard_map.136 = f32[576,512]{1,0:T(8,128)S(1)} custom-call(s32[1]{0:T(128)S(6)} %copy.16.shift, s32[4]{0:T(128)} %counts.1, f32[576,512]{1,0:T(8,128)} %tokens_in.1, bf16[512,1536]{1,0:T(8,128)(2,1)} %w_qkv.1, bf16[512,512]{1,0:T(8,128)(2,1)} %w_proj.1, bf16[512,2048]{1,0:T(8,128)(2,1)} %w_up.1, bf16[2048,512]{1,0:T(8,128)(2,1)} %w_down.1, ...), custom_call_target="tpu_custom_call" | custom-call | tf_op jit(solution)/shard_map/pallas_call | solution.py:602
  69.0 1.0 %copy.17 = f32[576,512]{1,0:T(8,128)} copy(f32[576,512]{1,0:T(8,128)S(1)} %shard_map.136) | data formatting | bytes 2359296

commit v6 on v5

--- a/solution.py
+++ b/solution.py
@@ -96,9 +96,13 @@
         return (((chip + way + chips) % chips) * 2 + core, head)
 
     barrier = pltpu.get_barrier_semaphore()
-    greeted = [before, after, partner, line(1), line(-1)] + plane[1:]
+    greeted = [before, after, partner] + plane[1:]
     for device in greeted:
         pl.semaphore_signal(barrier, inc=1, device_id=device, device_id_type=MESH)
+    for way in ways:
+        @pl.when((chip + way >= 0) & (chip + way < chips))
+        def _():
+            pl.semaphore_signal(barrier, inc=1, device_id=line(way), device_id_type=MESH)
 
     PROJ, QKV0, QKV1, UP0, UP1, DOWN = range(6)
     half_qkv, half_up = c_qkv.shape[0] // 2, c_up.shape[0] // 2
@@ -154,7 +158,7 @@
 
     token_load.wait()
     extended[WIN : WIN + rows, :] = norm(tokens[...]).astype(BF16)
-    pl.semaphore_wait(barrier, len(greeted))
+    pl.semaphore_wait(barrier, len(greeted) + 1 + (chip + chips - 1) // chips - (chip + 1) // chips)
 
     halo_left = remote(extended.at[pl.ds(WIN, WIN)], extended.at[pl.ds(WIN + rows, WIN)],
                        halo_send, halo_recv, before)

time: 70.2 us -> 70.3 us (level)
  no operation moved by 1% of the time
where the time goes in v6:
time: 70.3 us; the launch traced here: 70.2 us
  Pallas kernels  68.5 us (97%)
  local copies, waits for them, and re-layouts  1.02 us (1%)
    pallas_call x1, Pallas kernels, body(): pl.pallas_call(functools.partial(kernel, region_count, head_count), out_s...  68.5 us

profile of v6, /device:TPU:0, one launch (start us, length us, event | category | flops | bytes accessed | tf_op | source)
XLA Modules:
  0.0 70.2 jit_solution(4095155088257966323)
XLA Ops:
  0.7 68.5 %shard_map.136 = f32[576,512]{1,0:T(8,128)S(1)} custom-call(s32[1]{0:T(128)S(6)} %copy.16.shift, s32[4]{0:T(128)} %counts.1, f32[576,512]{1,0:T(8,128)} %tokens_in.1, bf16[512,1536]{1,0:T(8,128)(2,1)} %w_qkv.1, bf16[512,512]{1,0:T(8,128)(2,1)} %w_proj.1, bf16[512,2048]{1,0:T(8,128)(2,1)} %w_up.1, bf16[2048,512]{1,0:T(8,128)(2,1)} %w_down.1, ...), custom_call_target="tpu_custom_call" | custom-call | tf_op jit(solution)/shard_map/pallas_call | solution.py:606
  69.2 1.0 %copy.17 = f32[576,512]{1,0:T(8,128)} copy(f32[576,512]{1,0:T(8,128)S(1)} %shard_map.136) | data formatting | bytes 2359296
